TPU v7x, 256 devices: a whole 4x4x8 slice. The times are simulated.
256 devices in a mesh: sub: 64 (over x_hi, y, z), dom: 4 (over x_lo, core).
Axes of the slice: x: 4 (x_hi: 2, x_lo: 2; x = x_hi * 2 + x_lo), y: 4, z: 8, core: 2. Of those that a mesh axis runs over, the one named last changes fastest.
Arguments:
- source_points: float32 [1024, 3, 4096], P(('sub', 'dom')), may hold values from -4 to 4
- boundary: float32 [1024, 8, 6, 128], P(('sub', 'dom')), may hold values from -4 to 4, as said below
- poses: float32 [12, 1024], replicated, may hold values from -2 to 2, as said below
- anchor: float32 [1024], P(('sub', 'dom')), may hold values from 0.3 to 3
- edge_target: int32 [1024, 4], P(('sub', 'dom')), may hold values from 0 to 47, as said below
- corr_tile: int32 [1024, 4, 4], P(('sub', 'dom')), may hold values from 0 to 7
- corr_source: int32 [1024, 4, 4, 128], P(('sub', 'dom')), may hold values from 0 to 4095
- corr_lane: int32 [1024, 4, 4, 128], P(('sub', 'dom')), may hold values from 0 to 127
Outputs:
- refined_pose: float32 [12, 1024], P(None, ('sub', 'dom'))
Inputs may be any that keep to these rules, and one draw needn't show every extreme that they name: `poses`: each column holds a rotation matrix, row-major, followed by a translation. `boundary`: in every column of 6 entries the last 3 form a unit vector. `edge_target`: entry v of scan s names scan v % 16 of the previous (v // 16 = 0), the same (1) or the next (2) submap along the closed chain of submaps; it never names s itself; one scan may be named by several edges of s.
All inputs are finite; a program needn't handle non-finite values.
Results may differ from a plain program's by a relative error of at most 0.0001.
Values sent between devices are 32-bit elements; how exact they have to be, the bound alone decides.
A program may use at most 64 MiB of HBM per device.

v0:
```python
import jax
import jax.numpy as jnp
from jax import lax
from jax.sharding import Mesh
from jax.sharding import PartitionSpec as P

CG_ITERS = 2
GN_ITERS = 2
SUB_DOM = ("sub_0", "sub_1", "sub_2", "dom_0", "dom_1")
SUB = ("sub_0", "sub_1", "sub_2")
DOM = ("dom_0", "dom_1")


FINEST = lax.Precision.HIGHEST


def one_axis_at_a_time(value, axes):
    for axis in axes:
        value = lax.psum(value, axis)
    return value


def from_behind(block, axis, distance):
    devices = range(lax.axis_size(axis))
    route = [((i - distance) % len(devices), i) for i in devices]
    return lax.ppermute(block, axis, route)


def gather_turned(arrays, axis, dims):
    turned = [jnp.moveaxis(a, dim, 0) for a, dim in zip(arrays, dims)]
    widths = [t[0].size for t in turned]
    both = jnp.concatenate([t.reshape(-1, w) for t, w in zip(turned, widths)], axis=1)
    filled = lax.all_gather(both, axis, axis=0, tiled=True)
    tiles = jnp.split(filled, [sum(widths[:k]) for k in range(1, len(widths))], axis=1)
    return tuple(
        (
            jnp.moveaxis(b.reshape(-1, *t.shape[1:]), 0, dim)
            for b, t, dim in zip(tiles, turned, dims)
        )
    )


def split_up(value, dim, peers):
    before, after = (value.shape[:dim], value.shape[dim + 1 :])
    return jnp.moveaxis(value.reshape(*before, peers, -1, *after), dim, 0)


def sum_at_owner(value, axis, dim):
    peers = lax.axis_size(axis)
    tiles = lax.all_to_all(split_up(value, dim, peers), axis, 0, 0, tiled=True)
    return jnp.sum(tiles, axis=0)


def cayley(vector):
    first, second, third = (vector[0], vector[1], vector[2])
    length_sq = first * first + second * second + third * third
    inverse = 1.0 / (1.0 + length_sq)
    trace_part = 1.0 - length_sq
    entries = [
        [
            trace_part + 2.0 * first * first,
            2.0 * first * second - 2.0 * third,
            2.0 * first * third + 2.0 * second,
        ],
        [
            2.0 * first * second + 2.0 * third,
            trace_part + 2.0 * second * second,
            2.0 * second * third - 2.0 * first,
        ],
        [
            2.0 * first * third - 2.0 * second,
            2.0 * second * third + 2.0 * first,
            trace_part + 2.0 * third * third,
        ],
    ]
    return jnp.stack([jnp.stack(line) for line in entries]) * inverse


def rotate(matrix, vector):
    return jnp.stack(
        [
            matrix[row_id, 0] * vector[0]
            + matrix[row_id, 1] * vector[1]
            + matrix[row_id, 2] * vector[2]
            for row_id in range(3)
        ]
    )


def update(pose, increment):
    rotation = pose[:9].reshape(3, 3, -1)
    turn_mat = cayley(0.5 * increment[:3])
    rotated = jnp.stack(
        [
            jnp.stack(
                [
                    turn_mat[row_id, 0] * rotation[0, col_id]
                    + turn_mat[row_id, 1] * rotation[1, col_id]
                    + turn_mat[row_id, 2] * rotation[2, col_id]
                    for col_id in range(3)
                ]
            )
            for row_id in range(3)
        ]
    )
    moved_to = rotate(turn_mat, pose[9:]) + increment[3:]
    return jnp.concatenate([rotated.reshape(9, -1), moved_to], axis=0)


def scan_terms(points, pose_here, target_tiles, target_pose, sources, lane_ids):
    edge_count = sources.shape[0]
    picked = jnp.take(points, sources, axis=1)
    placed = rotate(pose_here[:9].reshape(3, 3), picked) + pose_here[9:, None, None, None]
    spread_lanes = jnp.broadcast_to(lane_ids[:, :, None, :], target_tiles.shape)
    chosen = jnp.take_along_axis(target_tiles, spread_lanes, axis=3)
    rotation = target_pose[:9].reshape(3, 3, edge_count)[:, :, :, None, None]
    shifted = target_pose[9:, :, None, None]
    target = (
        rotate(rotation, jnp.stack([chosen[:, :, 0], chosen[:, :, 1], chosen[:, :, 2]])) + shifted
    )
    normal = rotate(rotation, jnp.stack([chosen[:, :, 3], chosen[:, :, 4], chosen[:, :, 5]]))
    offset = target - placed
    misfit = normal[0] * offset[0] + normal[1] * offset[1] + normal[2] * offset[2]
    turned = jnp.stack(
        [
            placed[1] * normal[2] - placed[2] * normal[1],
            placed[2] * normal[0] - placed[0] * normal[2],
            placed[0] * normal[1] - placed[1] * normal[0],
        ]
    )
    jacobian = jnp.concatenate([turned, normal], axis=0).reshape(6, edge_count, -1)
    samples = jacobian.shape[2]
    blocks = jnp.einsum("aem,bem->eab", jacobian, jacobian, precision=FINEST) / samples
    slopes = (
        jnp.einsum("aem,em->ea", jacobian, misfit.reshape(edge_count, -1), precision=FINEST)
        / samples
    )
    return (blocks, slopes)


def window_order(sub_index, groups, scan_sub):
    slot_ids = (sub_index + jnp.arange(3, dtype=jnp.int32) - 1) % groups
    return (slot_ids[:, None] * scan_sub + jnp.arange(scan_sub, dtype=jnp.int32)[None, :]).reshape(
        -1
    )


def global_sum(value):
    return one_axis_at_a_time(value, SUB_DOM)


def spread_out(own_part):
    pieces = [from_behind(own_part, SUB, offset_by) for offset_by in (1, -1)]
    before, middle, beyond = gather_turned((pieces[0], own_part, pieces[1]), DOM, (1, 1, 1))
    nearby = jnp.concatenate([before, middle, beyond], axis=1)
    return nearby


def collect(partial_value):
    layers = partial_value.shape[0]
    scan_sub = partial_value.shape[2] // 3
    shared = sum_at_owner(partial_value.reshape(layers, 6, 3, scan_sub), DOM, 3)
    summed = shared[:, :, 1]
    for slot_id, offset_by in ((0, -1), (2, 1)):
        summed = summed + from_behind(shared[:, :, slot_id], SUB, offset_by)
    return summed


def local(source_points, boundary, poses, anchor, edge_target, corr_tile, corr_source, corr_lane):
    scan_dev = source_points.shape[0]
    edge_count = edge_target.shape[1]
    groups = lax.axis_size(SUB)
    scan_sub = scan_dev * lax.axis_size(DOM)
    sub_index = lax.axis_index(SUB)
    dom_index = lax.axis_index(DOM)
    window_index = window_order(sub_index, groups, scan_sub)
    middle = lax.all_gather(boundary, DOM, axis=0, tiled=True)
    pieces = [from_behind(middle, SUB, offset_by) for offset_by in (1, -1)]
    window_tiles = jnp.concatenate([pieces[0], middle, pieces[1]], axis=0)
    window_pose = jnp.take(poses, window_index, axis=1)
    own_start = scan_sub + dom_index * scan_dev
    source_at = (own_start + jnp.arange(scan_dev, dtype=jnp.int32))[:, None] + jnp.zeros(
        (1, edge_count), jnp.int32
    )
    from_end = source_at.reshape(-1)
    to_end = edge_target.reshape(-1)
    win_width = 3 * scan_sub
    for turn_id in range(GN_ITERS):
        own_pose = lax.dynamic_slice_in_dim(window_pose, own_start, scan_dev, 1)

        def per_scan(per_item, window_pose=window_pose):
            points, pose_here, targets, tile_ids, sources, lane_ids = per_item
            return scan_terms(
                points,
                pose_here,
                window_tiles[targets[:, None], tile_ids],
                jnp.take(window_pose, targets, axis=1),
                sources,
                lane_ids,
            )

        blocks, slopes = lax.map(
            per_scan, (source_points, own_pose.T, edge_target, corr_tile, corr_source, corr_lane)
        )
        blocks = blocks.reshape(-1, 6, 6)
        slopes = slopes.reshape(-1, 6)
        diag_terms = jnp.diagonal(blocks, axis1=1, axis2=2)
        empty = jnp.zeros((6, win_width), jnp.float32)
        right_part = empty.at[:, from_end].add(slopes.T).at[:, to_end].add(-slopes.T)
        diag_part = empty.at[:, from_end].add(diag_terms.T).at[:, to_end].add(diag_terms.T)
        totals = collect(jnp.stack([right_part, diag_part]))
        right_side = totals[0]
        diagonal_sum = totals[1] + anchor[None, :]

        def apply_system(vector, blocks=blocks):
            nearby = spread_out(vector)
            spread = nearby[:, from_end] - nearby[:, to_end]
            pushed = jnp.einsum("kab,bk->ak", blocks, spread, precision=FINEST)
            partial_value = (
                jnp.zeros((6, win_width), jnp.float32)
                .at[:, from_end]
                .add(pushed)
                .at[:, to_end]
                .add(-pushed)
            )
            return collect(partial_value[None])[0] + anchor[None, :] * vector

        residual = right_side
        scaled = residual / diagonal_sum
        direction = scaled
        energy = global_sum(jnp.sum(residual * scaled))
        increment = jnp.zeros((6, scan_dev), jnp.float32)
        for sweep in range(CG_ITERS):
            image = apply_system(direction)
            step_len = energy / global_sum(jnp.sum(direction * image))
            increment = increment + step_len * direction
            residual = residual - step_len * image
            if sweep + 1 < CG_ITERS:
                scaled = residual / diagonal_sum
                renewed = global_sum(jnp.sum(residual * scaled))
                direction = scaled + renewed / energy * direction
                energy = renewed
        window_pose = update(window_pose, spread_out(increment))
    return lax.dynamic_slice_in_dim(window_pose, own_start, scan_dev, 1)


def solution(mesh):
    split = Mesh(mesh.devices.reshape(2, 4, 8, 2, 2), ("sub_0", "sub_1", "sub_2", "dom_0", "dom_1"))
    return jax.shard_map(
        local,
        mesh=split,
        in_specs=(
            P(SUB_DOM, None, None),
            P(SUB_DOM, None, None, None),
            P(),
            P(SUB_DOM),
            P(SUB_DOM, None),
            P(SUB_DOM, None, None),
            P(SUB_DOM, None, None, None),
            P(SUB_DOM, None, None, None),
        ),
        out_specs=P(None, SUB_DOM),
        check_vma=False,
    )
```

profile of v0, /device:TPU:1, one launch (start us, length us, event | category | flops | bytes accessed | tf_op | source)
XLA Modules:
  0.0 1419.7 jit_solution(13061867911946272052)
XLA Ops:
  0.0 9.5 all_gather.21
  9.8 8.6 collective-permute-start.1
  29.3 440.6 %while.24 = (s32[]{:T(128)}, f32[4,4,6,6]{3,1,0,2:T(4,128)S(1)}, f32[4,4,6]{2,1,0:T(4,128)S(1)}, f32[4,12]{1,0:T(4,128)S(1)}, f32[4,3,4096]{1,2,0:T(8,128)}, /*i...) while((s32[]{:T(128)}, f32[4,4,6,6]{3,1,0,2:T(4,128)S(1)}, ...), condition=%wide.region_1.5_spmd, body=%wide.region_0.0_spmd.sunk | while | flops 1492314 | bytes 1967897 | solution.py:202
  45.4 91.5 %gather_fusion.1 = f32[12288]{0:T(1024)S(1)} fusion(f32[4,4,6,128]{3,2,1,0:T(8,128)S(1)} %bitcast.1285, s32[12288]{0:T(1024)S(1)} %reshape.2938), kind=kCustom, calls=%fused_computation.2.clone.clone.1 | custom fusion | bytes 294912 | tf_op jit(solution)/shard_map/while/body/eval_jaxpr/jit(take_along_axis)/gather | solution.py:115
  155.6 91.5 %gather_fusion.1 = f32[12288]{0:T(1024)S(1)} fusion(f32[4,4,6,128]{3,2,1,0:T(8,128)S(1)} %bitcast.1285, s32[12288]{0:T(1024)S(1)} %reshape.2938), kind=kCustom, calls=%fused_computation.2.clone.clone.1 | custom fusion | bytes 294912 | tf_op jit(solution)/shard_map/while/body/eval_jaxpr/jit(take_along_axis)/gather | solution.py:115
  265.7 91.5 %gather_fusion.1 = f32[12288]{0:T(1024)S(1)} fusion(f32[4,4,6,128]{3,2,1,0:T(8,128)S(1)} %bitcast.1285, s32[12288]{0:T(1024)S(1)} %reshape.2938), kind=kCustom, calls=%fused_computation.2.clone.clone.1 | custom fusion | bytes 294912 | tf_op jit(solution)/shard_map/while/body/eval_jaxpr/jit(take_along_axis)/gather | solution.py:115
  375.9 91.5 %gather_fusion.1 = f32[12288]{0:T(1024)S(1)} fusion(f32[4,4,6,128]{3,2,1,0:T(8,128)S(1)} %bitcast.1285, s32[12288]{0:T(1024)S(1)} %reshape.2938), kind=kCustom, calls=%fused_computation.2.clone.clone.1 | custom fusion | bytes 294912 | tf_op jit(solution)/shard_map/while/body/eval_jaxpr/jit(take_along_axis)/gather | solution.py:115
  482.4 7.3 collective-permute-start.2
  490.4 7.4 collective-permute-done.3
  497.9 7.2 collective-permute-start.5
  506.1 8.3 all-gather
  523.4 7.5 collective-permute-start.6
  531.7 7.4 collective-permute-done.7
  545.8 6.7 all-reduce.3
  552.5 11.7 all-reduce.1
  568.7 12.4 all-reduce.5
  589.0 8.3 psum.291
  597.3 13.1 psum.292
  614.8 11.2 psum.294
  627.2 7.2 collective-permute-start.9
  650.9 7.5 collective-permute-start.10
  659.2 7.4 collective-permute-done.11
  673.2 6.6 psum.296
  679.8 11.5 psum.297
  695.7 12.3 psum.299
  724.9 440.8 %while.25 = (s32[]{:T(128)}, f32[4,4,6,6]{3,1,0,2:T(4,128)S(1)}, f32[4,4,6]{2,1,0:T(4,128)S(1)}, f32[4,12]{1,0:T(4,128)S(1)}, f32[4,3,4096]{1,2,0:T(8,128)}, /*i...) while((s32[]{:T(128)}, f32[4,4,6,6]{3,1,0,2:T(4,128)S(1)}, ...), condition=%wide.region_38.42_spmd, body=%wide.region_37.41_spmd.sunk | while | flops 1492314 | bytes 1967897 | solution.py:202
  741.1 91.5 %gather_fusion.5 = f32[12288]{0:T(1024)S(1)} fusion(f32[4,4,6,128]{3,2,1,0:T(8,128)S(1)} %bitcast.1286, s32[12288]{0:T(1024)S(1)} %reshape.2951), kind=kCustom, calls=%fused_computation.6.clone.clone.1 | custom fusion | bytes 294912 | tf_op jit(solution)/shard_map/while/body/eval_jaxpr/jit(take_along_axis)/gather | solution.py:115
  851.3 91.5 %gather_fusion.5 = f32[12288]{0:T(1024)S(1)} fusion(f32[4,4,6,128]{3,2,1,0:T(8,128)S(1)} %bitcast.1286, s32[12288]{0:T(1024)S(1)} %reshape.2951), kind=kCustom, calls=%fused_computation.6.clone.clone.1 | custom fusion | bytes 294912 | tf_op jit(solution)/shard_map/while/body/eval_jaxpr/jit(take_along_axis)/gather | solution.py:115
  961.5 91.5 %gather_fusion.5 = f32[12288]{0:T(1024)S(1)} fusion(f32[4,4,6,128]{3,2,1,0:T(8,128)S(1)} %bitcast.1286, s32[12288]{0:T(1024)S(1)} %reshape.2951), kind=kCustom, calls=%fused_computation.6.clone.clone.1 | custom fusion | bytes 294912 | tf_op jit(solution)/shard_map/while/body/eval_jaxpr/jit(take_along_axis)/gather | solution.py:115
  1071.7 91.5 %gather_fusion.5 = f32[12288]{0:T(1024)S(1)} fusion(f32[4,4,6,128]{3,2,1,0:T(8,128)S(1)} %bitcast.1286, s32[12288]{0:T(1024)S(1)} %reshape.2951), kind=kCustom, calls=%fused_computation.6.clone.clone.1 | custom fusion | bytes 294912 | tf_op jit(solution)/shard_map/while/body/eval_jaxpr/jit(take_along_axis)/gather | solution.py:115
  1175.8 7.5 collective-permute-start.14
  1184.1 7.4 collective-permute-done.15
  1191.8 7.2 collective-permute-start.17
  1200.0 8.3 all-gather.3
  1217.3 7.5 collective-permute-start.18
  1225.6 7.4 collective-permute-done.19
  1239.7 6.6 all-reduce.2
  1246.3 11.5 all-reduce
  1262.2 12.4 all-reduce.4
  1282.5 8.3 psum.311
  1290.8 13.0 psum.312
  1308.3 11.2 psum.314
  1320.9 7.2 collective-permute-start.21
  1344.6 7.5 collective-permute-start.22
  1352.9 7.4 collective-permute-done.23
  1367.1 6.7 psum.316
  1373.7 11.5 psum.317
  1389.8 12.4 psum.319
  (604 shorter events, 336.9 us)
Async XLA Ops:
  0.0 26.4 %copy-start.4 = (s32[4,4]{1,0:T(4,128)S(1)}, s32[4,4]{1,0:T(4,128)}, u32[]{:S(2)}) copy-start(s32[4,4]{1,0:T(4,128)} %param.22) | copy-start | bytes 196
  9.5 18.1 %collective-permute-start = (f32[16,8,6,128]{3,1,2,0:T(8,128)S(1)}, f32[16,8,6,128]{3,1,2,0:T(8,128)S(1)}, u32[]{:S(2)}, u32[]{:S(2)}) collective-permute-start(f32[16,8,6,128]{3,1,2,0:T(8,128)S(1)} %all_gather.21), channel_id=1, source_target_pairs={{252,0},{0,4},{4,8},{8,12},{12,16},{16,20},{20,24},{24,28},{28,32}... | collective-permute-start | bytes 1179656 | tf_op jit(solution)/shard_map/ppermute | solution.py:26
  9.8 17.9 %collective-permute-start.1 = (f32[16,8,6,128]{3,1,2,0:T(8,128)S(1)}, f32[16,8,6,128]{3,1,2,0:T(8,128)S(1)}, u32[]{:S(2)}, u32[]{:S(2)}) collective-permute-start(f32[16,8,6,128]{3,1,2,0:T(8,128)S(1)} %all_gather.21), channel_id=1, source_target_pairs={{4,0},{8,4},{12,8},{16,12},{20,16},{24,20},{28,24},{32,28},{36,32}... | collective-permute-start | bytes 1179656 | tf_op jit(solution)/shard_map/ppermute | solution.py:26
  20.6 8.7 copy-start
  20.6 8.7 copy-start.1
  20.6 8.7 copy-start.3
  29.3 468.5 %copy-start.2 = (f32[4]{0:T(128)S(1)}, f32[4]{0:T(128)}, u32[]{:S(2)}) copy-start(f32[4]{0:T(128)} %param.21) | copy-start | bytes 52
  474.2 7.0 all-to-all-start
  482.4 8.0 collective-permute-start.2
  489.6 8.2 collective-permute-start.3
  497.9 8.2 collective-permute-start.4
  497.9 8.1 collective-permute-start.5
  523.4 8.3 collective-permute-start.6
  530.9 8.2 collective-permute-start.7
  627.2 8.2 collective-permute-start.8
  627.2 8.1 collective-permute-start.9
  650.9 8.3 collective-permute-start.10
  658.5 8.2 collective-permute-start.11
  709.2 8.2 collective-permute-start.12
  711.0 6.4 collective-permute-start.13
  1175.8 8.3 collective-permute-start.14
  1183.3 8.2 collective-permute-start.15
  1191.6 8.4 collective-permute-start.16
  1191.8 8.1 collective-permute-start.17
  1217.3 8.3 collective-permute-start.18
  1224.8 8.2 collective-permute-start.19
  1320.9 8.2 collective-permute-start.20
  1320.9 8.1 collective-permute-start.21
  1344.6 8.3 collective-permute-start.22
  1352.2 8.2 collective-permute-start.23
  1403.6 8.2 collective-permute-start.24
  1405.3 6.4 collective-permute-start.25
where the time goes:
time: 1420 us
  local copies, waits for them, and re-layouts  846 us (60%)
  blocking collectives  330 us (23%)
  starting transfers between devices  101 us (7%)
  other arithmetic  69.2 us (5%)
  waiting for transfers between devices  58.4 us (4%)
    gather x24, local copies, waits for them, and re-layouts, scan_terms(): chosen = jnp.take_along_axis(target_tiles, spread_lanes, axis=3)  732 us
    psum x30, blocking collectives, one_axis_at_a_time(): value = lax.psum(value, axis)  249 us
    ppermute x26, starting transfers between devices, from_behind(): return lax.ppermute(block, axis, route)  97.2 us
    ppermute x26, waiting for transfers between devices, from_behind(): return lax.ppermute(block, axis, route)  55.4 us
    gather x16, local copies, waits for them, and re-layouts, scan_terms(): picked = jnp.take(points, sources, axis=1)  46.4 us
    add x26, other arithmetic, rotate(): matrix[row_id, 0] * vector[0] + matrix[row_id, 1] * vector[1]  45.4 us
    all_gather x6, blocking collectives, gather_turned(): filled = lax.all_gather(both, axis, axis=0, tiled=True)  42.6 us
  transfers between devices with their start and end apart: 27, of which 20 were waited for; matrix products, arithmetic and copies ran while one was open for 1% of the time, Pallas kernels for 0%

commit v1 on v0

v1 whole, which is shorter than its diff:
```python
import functools

import jax
import jax.numpy as jnp
from jax import lax
from jax.experimental import pallas as pl
from jax.experimental.pallas import tpu as pltpu
from jax.sharding import PartitionSpec as P

MESH = pl.DeviceIdType.MESH
F32 = jnp.float32
BF16 = jnp.bfloat16
GN_ITERS = 2
SCAN_DEV = 4
EDGE_SCAN = 4
CT = 4
EDGES = SCAN_DEV * EDGE_SCAN
REACH = 3
SLOTS = 2 * REACH + 1
TILES = 4 * SLOTS
PAD = 32
SAMPLES = CT * 128
PAIRS = [(a, b) for a in range(6) for b in range(a, 6)]


def iota(shape, dim):
    return lax.broadcasted_iota(jnp.int32, shape, dim)


def parts_of(value):
    first = value.astype(BF16)
    rest = value - first.astype(F32)
    second = rest.astype(BF16)
    third = (rest - second.astype(F32)).astype(BF16)
    return (third, second, first)


def dot(a, b):
    return jnp.dot(a, b, preferred_element_type=F32)


def pick_left(select, value):
    third, second, first = parts_of(value)
    return (dot(select, third) + dot(select, second)) + dot(select, first)


def pick_right(value, select):
    third, second, first = parts_of(value)
    return (dot(third, select) + dot(second, select)) + dot(first, select)


def pick_turned(select, value):
    turned = (((1,), (1,)), ((), ()))
    third, second, first = [
        lax.dot_general(select, part, turned, preferred_element_type=F32)
        for part in parts_of(value)
    ]
    return (third + second) + first


def cayley(first, second, third):
    length_sq = first * first + second * second + third * third
    inverse = 1.0 / (1.0 + length_sq)
    trace_part = 1.0 - length_sq
    entries = [
        trace_part + 2.0 * first * first,
        2.0 * first * second - 2.0 * third,
        2.0 * first * third + 2.0 * second,
        2.0 * first * second + 2.0 * third,
        trace_part + 2.0 * second * second,
        2.0 * second * third - 2.0 * first,
        2.0 * first * third - 2.0 * second,
        2.0 * second * third + 2.0 * first,
        trace_part + 2.0 * third * third,
    ]
    return [entry * inverse for entry in entries]


def kernel(
    groups,
    source_ref,
    boundary_ref,
    poses_ref,
    anchor_ref,
    target_ref,
    tile_ref,
    corr_source_ref,
    corr_lane_ref,
    out_ref,
    window,
    early,
    early_own,
    gram,
    gram_own,
    near,
    near_own,
    far,
    far_own,
    picked,
    chosen,
    comps,
    ends,
    win_send,
    win_recv,
    early_send,
    early_recv,
    gram_send,
    gram_recv,
    near_send,
    near_recv,
    far_send,
    far_recv,
    local_sem,
):
    sub = lax.axis_index("sub")
    dom = lax.axis_index("dom")
    half_groups = groups // 2
    sub_low = lax.rem(sub, half_groups)
    sub_high = sub // half_groups

    def near_by(offset):
        return lax.rem(sub + offset + groups, groups)

    window_partners = []
    halo_partners = []
    for offset in range(-REACH, REACH + 1):
        for turn in range(4):
            if offset == 0 and turn == 0:
                continue
            other = lax.rem(dom + turn, 4)
            device = (near_by(offset), other)
            halo_partners.append(
                (device, (REACH - offset) * 4 + dom, (REACH + offset) * 4 + other)
            )
            if abs(offset) <= 1:
                window_partners.append(
                    (device, (1 - offset) * 4 + dom, (1 + offset) * 4 + other)
                )
    near_partners = []
    for turn in range(1, 8):
        spot = lax.rem(sub_high * 4 + dom + turn, 8)
        device = ((spot // 4) * half_groups + sub_low, lax.rem(spot, 4))
        near_partners.append((device, sub_high * 4 + dom, spot))
    far_partners = []
    for turn in range(1, half_groups):
        spot = lax.rem(sub_low + turn, half_groups)
        far_partners.append(((sub_high * half_groups + spot, dom), sub_low, spot))

    barrier = pltpu.get_barrier_semaphore()
    everyone = halo_partners + near_partners + far_partners
    for device, _, _ in everyone:
        pl.semaphore_signal(barrier, inc=1, device_id=device, device_id_type=MESH)

    own_tiles = pltpu.make_async_copy(
        boundary_ref, window.at[pl.ds((4 + dom) * 32, 32)], local_sem
    )
    own_tiles.start()
    lane_row = iota((1, 128), 1)
    row = jnp.zeros((1, 128), F32)
    edge_of_row = iota((EDGES, 128), 0)
    own_target = jnp.zeros((EDGES, 128), jnp.int32)
    for edge in range(EDGES):
        value = target_ref[edge // EDGE_SCAN, edge % EDGE_SCAN]
        row = jnp.where(lane_row == edge, value.astype(F32), row)
        own_target = jnp.where(edge_of_row == edge, value, own_target)
    for scan in range(SCAN_DEV):
        row = jnp.where(lane_row == EDGES + scan, anchor_ref[scan], row)
    early_own[0] = row
    early[pl.ds(REACH * 4 + dom, 1)] = row.reshape(1, 1, 128)
    early[pl.ds(TILES, PAD - TILES)] = jnp.zeros((PAD - TILES, 1, 128), F32)
    for step in range(GN_ITERS):
        gram[step, pl.ds(TILES, PAD - TILES)] = jnp.zeros((PAD - TILES, 8, 128), F32)

    pl.semaphore_wait(barrier, len(everyone))

    def push(source, at_partner, here, send_sem, recv_sem, partners):
        copies = []
        for number, (device, mine, theirs) in enumerate(partners):
            copy = pltpu.make_async_remote_copy(
                src_ref=source,
                dst_ref=at_partner(mine),
                send_sem=send_sem(number),
                recv_sem=recv_sem(mine),
                device_id=device,
                device_id_type=MESH,
            )
            copy.start()
            arrival = pltpu.make_async_remote_copy(
                src_ref=source,
                dst_ref=here(theirs),
                send_sem=send_sem(number),
                recv_sem=recv_sem(theirs),
                device_id=device,
                device_id_type=MESH,
            )
            copies.append((copy, arrival))
        return copies

    started = []
    tile_slot = lambda slot: window.at[pl.ds(slot * 32, 32)]
    window_copies = push(
        boundary_ref,
        tile_slot,
        tile_slot,
        lambda n: win_send.at[n],
        lambda n: win_recv.at[n],
        window_partners,
    )
    early_slot = lambda slot: early.at[pl.ds(slot, 1)]
    early_copies = push(
        early_own,
        early_slot,
        early_slot,
        lambda n: early_send.at[n],
        lambda n: early_recv.at[n],
        halo_partners,
    )
    started += window_copies + early_copies

    def gather_scan(scan, carry):
        indices = corr_source_ref[scan].reshape(EDGE_SCAN * CT, 128)
        low = lax.bitwise_and(indices, 127)
        high = lax.shift_right_logical(indices, 7)
        found = [jnp.zeros((EDGE_SCAN * CT, 128), F32) for _ in range(3)]
        for block in range(32):
            here = high == block
            for comp in range(3):
                line = source_ref[scan, pl.ds(comp, 1), pl.ds(block * 128, 128)]
                wide = jnp.broadcast_to(line, (EDGE_SCAN * CT, 128))
                value = jnp.take_along_axis(wide, low, axis=1, mode="promise_in_bounds")
                found[comp] = jnp.where(here, value, found[comp])
        for comp in range(3):
            picked[comp, pl.ds(scan * 16, 16), :] = found[comp]
        return carry

    lax.fori_loop(0, SCAN_DEV, gather_scan, 0)

    start = near_by(-REACH) * 16
    first_tile = start // 128
    next_tile = lax.rem(first_tile + 1, groups * 16 // 128)
    pair = jnp.concatenate(
        [
            poses_ref[:, pl.ds(pl.multiple_of(first_tile * 128, 128), 128)],
            poses_ref[:, pl.ds(pl.multiple_of(next_tile * 128, 128), 128)],
        ],
        axis=1,
    )
    shift = lax.rem(256 - lax.rem(start, 128), 256)
    rolled = pltpu.roll(pair, shift, 1)[:, :128]
    pose = [rolled[k : k + 1] for k in range(12)]

    lane16 = iota((EDGES, 128), 1)
    own_source_lane = REACH * 16 + dom * SCAN_DEV + edge_of_row // EDGE_SCAN
    own_ends = jnp.concatenate(
        [
            (lane16 == own_source_lane).astype(F32),
            (lane16 == own_target + (REACH - 1) * 16).astype(F32),
        ],
        axis=0,
    ).astype(BF16)

    from_lane = iota((128, 128), 0)
    to_lane = iota((128, 128), 1)
    from_a = lax.shift_right_logical(from_lane, 3) & 7
    from_b = from_lane & 7
    to_half = lax.shift_right_logical(to_lane, 6)
    to_a = lax.shift_right_logical(to_lane, 3) & 7
    to_b = to_lane & 7
    used = (to_a < 6) & (to_b < 6) & (from_b < 6)
    as_select = lambda mask: mask.astype(F32).astype(BF16)
    over_b = as_select(used & (from_a == to_b))
    slopes_out = as_select(used & (from_a == 6) & (from_b == to_b))
    diagonal_out = as_select(used & (from_a == from_b) & (from_b == to_b))
    left = to_half == 0
    left_256 = iota((256, 128), 1) < 64

    for _, arrival in early_copies:
        arrival.wait_recv()
    rows = early[...].reshape(PAD, 128)
    rows_turned = jnp.concatenate([rows, jnp.zeros((128 - PAD, 128), F32)], axis=0).T
    lane8 = iota((8, 128), 1)
    row8 = iota((8, 128), 0)
    for tile in range(TILES):
        for half in range(2):
            target = rows_turned[half * 8 : half * 8 + 8, tile : tile + 1]
            target_lane = target + float((tile // 4 - 1) * 16)
            source_lane = tile * 4 + half * 2 + row8 // 4
            ends[pl.ds(tile * 8, 8), pl.ds(half * 128, 128)] = (
                lane8 == source_lane
            ).astype(F32) - (lane8.astype(F32) == target_lane).astype(F32)
    ends[pl.ds(TILES * 8, (PAD - TILES) * 8), :] = jnp.zeros(((PAD - TILES) * 8, 256), F32)
    ends_f32 = ends[...]
    ends_turned_f32 = ends_f32.T
    ends_in = ends_f32.astype(BF16)
    ends_out = ends_turned_f32.astype(BF16)
    ends_abs = jnp.abs(ends_turned_f32).astype(BF16)
    node = iota((128, PAD), 0)
    of_tile = as_select(node // 4 == iota((128, PAD), 1))
    anchor_rows = pick_left(of_tile, rows)
    node_128 = from_lane
    mine = to_lane == EDGES + (node_128 & 3)
    anchor = jnp.sum(jnp.where(mine, anchor_rows, 0.0), axis=1, keepdims=True)
    anchor = jnp.where(node_128 < TILES * 4, jnp.broadcast_to(anchor, (128, 128)), 1.0)
    own_nodes = (
        (node_128 // 4 == REACH * 4 + dom)
        & (to_lane < 6)
    )

    own_tiles.wait()
    for _, arrival in window_copies:
        arrival.wait_recv()

    def gather_edge(edge, carry):
        scan = edge // EDGE_SCAN
        slot = lax.rem(edge, EDGE_SCAN)
        first = target_ref[scan, slot] * 8
        lanes = corr_lane_ref[scan, slot]
        for chunk in range(CT):
            tile = window[first + tile_ref[scan, slot, chunk]]
            spread = jnp.broadcast_to(lanes[chunk : chunk + 1], (8, 128))
            value = jnp.take_along_axis(tile, spread, axis=1, mode="promise_in_bounds")
            chosen[pl.ds(pl.multiple_of(edge * 32 + chunk * 8, 8), 8), :] = value
        return carry

    lax.fori_loop(0, EDGES, gather_edge, 0)
    for chunk in range(CT):
        for comp in range(3):
            comps[comp, chunk] = picked[comp, pl.ds(chunk, EDGES, stride=CT), :]
        for comp in range(6):
            comps[3 + comp, chunk] = chosen[pl.ds(chunk * 8 + comp, EDGES, stride=32), :]

    msg_pos = lane8 & 63

    for step in range(GN_ITERS):
        pose_rows = jnp.concatenate(pose + [jnp.zeros((4, 128), F32)], axis=0)
        pose_ends = pick_turned(own_ends, pose_rows)
        message = jnp.zeros((8, 128), F32)
        for half in range(2):
            here = [
                jnp.broadcast_to(pose_ends[half * 8 : half * 8 + 8, k : k + 1], (8, 128))
                for k in range(12)
            ]
            there = [
                jnp.broadcast_to(
                    pose_ends[EDGES + half * 8 : EDGES + half * 8 + 8, k : k + 1], (8, 128)
                )
                for k in range(12)
            ]
            sums = {}
            for chunk in range(CT):
                data = [comps[k, chunk, pl.ds(half * 8, 8), :] for k in range(9)]

                def turn(matrix, vector):
                    return [
                        matrix[3 * i] * vector[0]
                        + matrix[3 * i + 1] * vector[1]
                        + matrix[3 * i + 2] * vector[2]
                        for i in range(3)
                    ]

                placed = [v + t for v, t in zip(turn(here[:9], data[0:3]), here[9:])]
                target = [v + t for v, t in zip(turn(there[:9], data[3:6]), there[9:])]
                normal = turn(there[:9], data[6:9])
                offset = [q - p for q, p in zip(target, placed)]
                misfit = normal[0] * offset[0] + normal[1] * offset[1] + normal[2] * offset[2]
                jac = [
                    placed[1] * normal[2] - placed[2] * normal[1],
                    placed[2] * normal[0] - placed[0] * normal[2],
                    placed[0] * normal[1] - placed[1] * normal[0],
                ] + normal
                for a, b in PAIRS:
                    term = jac[a] * jac[b]
                    sums[a, b] = sums[a, b] + term if chunk else term
                for b in range(6):
                    term = jac[b] * misfit
                    sums[6, b] = sums[6, b] + term if chunk else term
            in_half = lane8 // 64 == half
            for (a, b), value in sums.items():
                total = jnp.sum(value, axis=1, keepdims=True) * (1.0 / SAMPLES)
                place = msg_pos == a * 8 + b
                if a < 6:
                    place = place | (msg_pos == b * 8 + a)
                message = jnp.where(in_half & place, total, message)
        gram_own[step, 0] = message
        gram[step, pl.ds(REACH * 4 + dom, 1)] = message.reshape(1, 8, 128)
        gram_slot = lambda slot: gram.at[step, pl.ds(slot, 1)]
        gram_copies = push(
            gram_own.at[step],
            gram_slot,
            gram_slot,
            lambda n: gram_send.at[step, n],
            lambda n: gram_recv.at[step, n],
            halo_partners,
        )
        started += gram_copies
        for _, arrival in gram_copies:
            arrival.wait_recv()
        terms = gram[step].reshape(PAD * 8, 128)

        def at_nodes(select, value):
            both = pick_left(select, value)
            return jnp.where(left, both[:128], both[128:])

        def difference(select, value):
            twice = jnp.concatenate([value, value], axis=0)
            sides = iota((256, 128), 0) < 128
            return pick_left(select, jnp.where(sides == left_256, twice, 0.0))

        def apply_system(value):
            image = at_nodes(ends_out, terms * difference(ends_in, value))
            return pick_right(image, over_b) + anchor * value

        residual = pick_right(at_nodes(ends_out, terms), slopes_out)
        diagonal = pick_right(at_nodes(ends_abs, terms), diagonal_out) + anchor
        inverse = 1.0 / diagonal
        scaled = residual * inverse
        image = apply_system(scaled)
        second = image * inverse

        own_in = jnp.concatenate(
            [
                ends[pl.ds(pl.multiple_of((REACH * 4 + dom) * 8, 8), 8), :],
                jnp.zeros((8, 256), F32),
            ],
            axis=0,
        ).astype(BF16)
        own_diff = difference(own_in, second)
        first_row = as_select(
            (lax.shift_right_logical(from_lane, 6) == to_half)
            & (from_a == 0)
            & (from_b == to_a)
            & (to_a < 6)
        )
        own_diff_a = pick_right(own_diff, first_row)
        quad = (message * own_diff[:8]) * own_diff_a[:8]

        def inner(a, b):
            return jnp.sum(jnp.where(own_nodes, a * b, 0.0), keepdims=True)

        energy = inner(residual, scaled)
        curve = inner(scaled, image)
        cross = inner(second, image)
        bend = inner(anchor * second, second) + jnp.sum(quad, keepdims=True)
        sums_row = jnp.zeros((1, 128), F32)
        for number, value in enumerate((energy, curve, cross, bend)):
            sums_row = jnp.where(lane_row == number, value, sums_row)

        def exchange(value, own, buffer, spot, count, send, recv, partners):
            own[step, 0] = value
            buffer[step, pl.ds(spot, 1)] = value.reshape(1, 1, 128)
            slot = lambda n: buffer.at[step, pl.ds(n, 1)]
            copies = push(
                own.at[step],
                slot,
                slot,
                lambda n: send.at[step, n],
                lambda n: recv.at[step, n],
                partners,
            )
            for _, arrival in copies:
                arrival.wait_recv()
            gathered = buffer[step].reshape(count, 128)
            return copies, jnp.sum(gathered, axis=0, keepdims=True)

        scaled_turned = scaled.T[:8]
        second_turned = second.T[:8]
        copies, sums_row = exchange(
            sums_row, near_own, near, sub_high * 4 + dom, 8, near_send, near_recv, near_partners
        )
        started += copies
        copies, sums_row = exchange(
            sums_row, far_own, far, sub_low, half_groups, far_send, far_recv, far_partners
        )
        started += copies

        energy, curve, cross, bend = [sums_row[:, k : k + 1] for k in range(4)]
        step_one = energy / curve
        renewed = step_one * step_one * cross - energy
        ratio = renewed / energy
        curve_two = (
            curve
            - 2.0 * step_one * cross
            + step_one * step_one * bend
            + 2.0 * ratio * (curve - step_one * cross)
            + ratio * ratio * curve
        )
        step_two = renewed / curve_two
        increment = (step_one + step_two * (1.0 + ratio)) * scaled_turned - (
            step_two * step_one
        ) * second_turned
        inc = [increment[k : k + 1] for k in range(6)]
        turn_mat = cayley(0.5 * inc[0], 0.5 * inc[1], 0.5 * inc[2])
        rotated = [
            turn_mat[3 * i] * pose[j]
            + turn_mat[3 * i + 1] * pose[3 + j]
            + turn_mat[3 * i + 2] * pose[6 + j]
            for i in range(3)
            for j in range(3)
        ]
        moved = [
            turn_mat[3 * i] * pose[9]
            + turn_mat[3 * i + 1] * pose[10]
            + turn_mat[3 * i + 2] * pose[11]
            + inc[3 + i]
            for i in range(3)
        ]
        pose = rotated + moved

    final = jnp.concatenate(pose + [jnp.zeros((4, 128), F32)], axis=0)
    final = pltpu.roll(final, 128 - (REACH * 16 + dom * SCAN_DEV), 1)
    out_ref[...] = final[:12, :SCAN_DEV]

    for copy, _ in started:
        copy.wait_send()


def local(groups, source_points, boundary, poses, anchor, edge_target, corr_tile, corr_source, corr_lane):
    vmem = pl.BlockSpec(memory_space=pltpu.VMEM)
    smem = pl.BlockSpec(memory_space=pltpu.SMEM)
    dma = pltpu.SemaphoreType.DMA
    halo = TILES - 1
    far = groups // 2
    return pl.pallas_call(
        functools.partial(kernel, groups),
        out_shape=jax.ShapeDtypeStruct((12, SCAN_DEV), F32),
        in_specs=[vmem, vmem, vmem, smem, smem, smem, vmem, vmem],
        out_specs=vmem,
        scratch_shapes=[
            pltpu.VMEM((12 * 32, 8, 128), F32),
            pltpu.VMEM((PAD, 1, 128), F32),
            pltpu.VMEM((1, 1, 128), F32),
            pltpu.VMEM((GN_ITERS, PAD, 8, 128), F32),
            pltpu.VMEM((GN_ITERS, 1, 8, 128), F32),
            pltpu.VMEM((GN_ITERS, 8, 1, 128), F32),
            pltpu.VMEM((GN_ITERS, 1, 1, 128), F32),
            pltpu.VMEM((GN_ITERS, far, 1, 128), F32),
            pltpu.VMEM((GN_ITERS, 1, 1, 128), F32),
            pltpu.VMEM((3, 64, 128), F32),
            pltpu.VMEM((512, 128), F32),
            pltpu.VMEM((9, CT, EDGES, 128), F32),
            pltpu.VMEM((PAD * 8, 256), F32),
            dma((11,)),
            dma((12,)),
            dma((halo,)),
            dma((TILES,)),
            dma((GN_ITERS, halo)),
            dma((GN_ITERS, TILES)),
            dma((GN_ITERS, 7)),
            dma((GN_ITERS, 8)),
            dma((GN_ITERS, far - 1)),
            dma((GN_ITERS, far)),
            dma,
        ],
        compiler_params=pltpu.CompilerParams(collective_id=0, has_side_effects=True),
    )(
        source_points,
        jnp.pad(boundary.reshape(32, 6, 128), ((0, 0), (0, 2), (0, 0))),
        poses,
        anchor,
        edge_target,
        corr_tile,
        corr_source,
        corr_lane,
    )


def solution(mesh):
    both = ("sub", "dom")
    return jax.shard_map(
        functools.partial(local, mesh.shape["sub"]),
        mesh=mesh,
        in_specs=(
            P(both, None, None),
            P(both, None, None, None),
            P(),
            P(both),
            P(both, None),
            P(both, None, None),
            P(both, None, None, None),
            P(both, None, None, None),
        ),
        out_specs=P(None, both),
        check_vma=False,
    )
```

time: 1420 us -> 77.1 us (0.05)
  local copies, waits for them, and re-layouts: 846 us -> 3.81 us
  blocking collectives: 330 us -> 0 us
  starting transfers between devices: 101 us -> 0 us
  Pallas kernels: 0 us -> 73.1 us
  other arithmetic: 69.2 us -> 0 us
  waiting for transfers between devices: 58.4 us -> 0 us
    gather x68 -> x0, local copies, waits for them, and re-layouts: 805 us -> none  [the longest x24 732 us: scan_terms(): chosen = jnp.take_along_axis(target_tiles, spread_lanes, axis=3)]
    psum x30 -> x0, blocking collectives: 249 us -> none  [one_axis_at_a_time(): value = lax.psum(value, axis)]
    ppermute x26 -> x0, starting transfers between devices: 97.2 us -> none  [from_behind(): return lax.ppermute(block, axis, route)]
    pallas_call x0 -> x1, Pallas kernels: none -> 73.1 us  [local(): pl.pallas_call(functools.partial(kernel, groups), out_shape=jax.ShapeDtyp...]
    ppermute x26 -> x0, waiting for transfers between devices: 55.4 us -> none  [from_behind(): return lax.ppermute(block, axis, route)]
    all_gather x7 -> x0, blocking collectives: 52.1 us -> none  [the longest x6 42.6 us: gather_turned(): filled = lax.all_gather(both, axis, axis=0, tiled=True)]
    add x60 -> x0, other arithmetic: 46.6 us -> none  [the longest x26 45.4 us: rotate(): matrix[row_id, 0] * vector[0] + matrix[row_id, 1] * vector[1]]
    all_to_all x5 -> x0, blocking collectives: 28.2 us -> none  [sum_at_owner(): tiles = lax.all_to_all(split_up(value, dim, peers), axis, 0, 0, tiled=True)]
  transfers between devices with their start and end apart: 27 -> 0, of which waited for: 20 -> 0; matrix products, arithmetic and copies ran while one was open for 1% -> 0% of each run, Pallas kernels for 0% -> 0%
where the time goes in v1:
time: 77.1 us; the launch traced here: 76.9 us
  Pallas kernels  73.1 us (95%)
  local copies, waits for them, and re-layouts  3.81 us (5%)
    pallas_call x1, Pallas kernels, local(): pl.pallas_call(functools.partial(kernel, groups), out_shape=jax.ShapeDtyp...  73.1 us
    unnamed x4, local copies, waits for them, and re-layouts  1.79 us

profile of v1, /device:TPU:1, one launch (start us, length us, event | category | flops | bytes accessed | tf_op | source)
XLA Modules:
  0.0 76.9 jit_solution(1722904173209795111)
XLA Ops:
  0.0 0.0 copy-start
  0.0 1.0 %copy.9 = f32[4,8,6,128]{3,2,1,0:T(8,128)S(1)} copy(f32[4,8,6,128]{3,1,2,0:T(8,128)} %param.9) | data formatting | bytes 196608 | tf_op args[1]
  1.0 0.7 pad.4.boundary_ref
  1.6 0.0 copy-done
  1.6 0.8 %copy.10.source_ref = f32[4,3,4096]{2,1,0:T(4,128)} copy(f32[4,3,4096]{2,0,1:T(4,128)S(1)} %copy-done) | data formatting | bytes 393216 | tf_op args[0]
  2.5 73.1 %shard_map.82 = f32[12,4]{1,0:T(8,128)} custom-call(f32[4,3,4096]{2,1,0:T(4,128)} %copy.10.source_ref, f32[32,8,128]{2,1,0:T(8,128)} %pad.4.boundary_ref, f32[12,1024]{1,0:T(8,128)} %poses_ref.1, f32[4]{0:T(128)} %anchor_ref.1, s32[4,4]{1,0:T(4,128)} %target_ref.1, s32[4,4,4]{2,1,0:T(4,128)} %tile_ref.1, s32[4,4,4,128]{3,2,1,0:T(4,128)} %corr_source_ref.1, ...), custom_call_target="tpu_custom_call" | custom-call | tf_op jit(solution)/shard_map/pallas_call | solution.py:523
  75.6 1.4 %copy.11 = f32[12,4]{0,1:T(4,128)} copy(f32[12,4]{1,0:T(8,128)} %shard_map.82) | data formatting | bytes 384 | tf_op jit(solution)/shard_map/pallas_call | solution.py:523
Async XLA Ops:
  0.0 1.6 %copy-start = (f32[4,3,4096]{2,0,1:T(4,128)S(1)}, f32[4,3,4096]{2,0,1:T(4,128)}, u32[]{:S(2)}) copy-start(f32[4,3,4096]{2,0,1:T(4,128)} %param.8) | copy-start | bytes 589828

commit v2 on v1

--- a/solution.py
+++ b/solution.py
@@ -20,6 +20,9 @@
 TILES = 4 * SLOTS
 PAD = 32
 SAMPLES = CT * 128
+ROWS = SCAN_DEV * 6 * 8
+PARTS = 2
+PART = ROWS // PARTS
 PAIRS = [(a, b) for a in range(6) for b in range(a, 6)]
 
 
@@ -78,24 +81,23 @@
 
 def kernel(
     groups,
-    source_ref,
-    boundary_ref,
-    poses_ref,
+    source_hbm,
+    boundary_hbm,
+    poses_hbm,
     anchor_ref,
     target_ref,
     tile_ref,
+    corr_source_hbm,
+    corr_lane_hbm,
+    out_ref,
     corr_source_ref,
     corr_lane_ref,
-    out_ref,
+    source_ref,
+    poses_ref,
     window,
     early,
-    early_own,
     gram,
-    gram_own,
-    near,
-    near_own,
     far,
-    far_own,
     picked,
     chosen,
     comps,
@@ -106,11 +108,9 @@
     early_recv,
     gram_send,
     gram_recv,
-    near_send,
-    near_recv,
     far_send,
     far_recv,
-    local_sem,
+    load_sem,
 ):
     sub = lax.axis_index("sub")
     dom = lax.axis_index("dom")
@@ -121,40 +121,129 @@
     def near_by(offset):
         return lax.rem(sub + offset + groups, groups)
 
-    window_partners = []
-    halo_partners = []
-    for offset in range(-REACH, REACH + 1):
-        for turn in range(4):
-            if offset == 0 and turn == 0:
-                continue
-            other = lax.rem(dom + turn, 4)
-            device = (near_by(offset), other)
-            halo_partners.append(
-                (device, (REACH - offset) * 4 + dom, (REACH + offset) * 4 + other)
+    halo_partners = [
+        ((near_by(offset), lax.bitwise_xor(dom, other)), (REACH - offset) * 4 + dom)
+        for distance in range(REACH + 1)
+        for offset in ((distance, -distance) if distance else (0,))
+        for other in range(4)
+        if distance or other
+    ]
+    sum_partners = [
+        ((sub_high * half_groups + lax.rem(sub_low + turn, half_groups), dom), sub)
+        for turn in range(1, half_groups)
+    ] + [
+        (
+            (
+                (1 - sub_high) * half_groups + lax.rem(sub_low + turn, half_groups),
+                lax.bitwise_xor(dom, 2),
+            ),
+            sub,
+        )
+        for turn in range(half_groups)
+    ]
+
+    loads = [
+        pltpu.make_async_copy(source, target, load_sem.at[number])
+        for number, (source, target) in enumerate(
+            (
+                (boundary_hbm, window.at[pl.ds((4 + dom) * ROWS, ROWS)]),
+                (corr_source_hbm, corr_source_ref),
+                (source_hbm, source_ref),
+                (poses_hbm, poses_ref),
+                (corr_lane_hbm, corr_lane_ref),
             )
-            if abs(offset) <= 1:
-                window_partners.append(
-                    (device, (1 - offset) * 4 + dom, (1 + offset) * 4 + other)
-                )
-    near_partners = []
-    for turn in range(1, 8):
-        spot = lax.rem(sub_high * 4 + dom + turn, 8)
-        device = ((spot // 4) * half_groups + sub_low, lax.rem(spot, 4))
-        near_partners.append((device, sub_high * 4 + dom, spot))
-    far_partners = []
-    for turn in range(1, half_groups):
-        spot = lax.rem(sub_low + turn, half_groups)
-        far_partners.append(((sub_high * half_groups + spot, dom), sub_low, spot))
-
+        )
+    ]
+    for load in loads:
+        load.start()
     barrier = pltpu.get_barrier_semaphore()
-    everyone = halo_partners + near_partners + far_partners
-    for device, _, _ in everyone:
+    everyone = halo_partners + sum_partners
+    for device, _ in everyone:
         pl.semaphore_signal(barrier, inc=1, device_id=device, device_id_type=MESH)
 
-    own_tiles = pltpu.make_async_copy(
-        boundary_ref, window.at[pl.ds((4 + dom) * 32, 32)], local_sem
-    )
-    own_tiles.start()
+    pl.semaphore_wait(barrier, len(everyone))
+
+    def push(copies, send_sem, recv_sem):
+        for source, target, device in copies:
+            pltpu.make_async_remote_copy(
+                src_ref=source,
+                dst_ref=target,
+                send_sem=send_sem,
+                recv_sem=recv_sem,
+                device_id=device,
+                device_id_type=MESH,
+            ).start()
+
+    def whole(ref, send_sem, recv_sem):
+        return pltpu.make_async_remote_copy(
+            src_ref=ref,
+            dst_ref=ref,
+            send_sem=send_sem,
+            recv_sem=recv_sem,
+            device_id=(sub, lax.bitwise_xor(dom, 1)),
+            device_id_type=MESH,
+        )
+
+    own_slot = REACH * 4 + dom
+
+    def halo_push(buffer, send, recv):
+        own = buffer.at[pl.ds(own_slot, 1)]
+        push(
+            [(own, buffer.at[pl.ds(slot, 1)], device) for device, slot in halo_partners],
+            send,
+            recv,
+        )
+        return whole(buffer.at[pl.ds(0, TILES - 1)], send, recv)
+
+    started = []
+    loads[0].wait()
+    sibling = lax.bitwise_xor(dom, 1)
+    across = lax.bitwise_xor(dom, 2)
+    to_sibling = (sub, sibling)
+    to_across = (sub, across)
+
+    to_next = lax.bitwise_xor(dom, 2 * (sub_low // (half_groups - 1)))
+    to_last = lax.bitwise_xor(dom, 2 * (lax.rem(sub_low + half_groups - 1, half_groups) // (half_groups - 1)))
+
+    def window_copy(number, part, slot, device):
+        at = window.at[pl.ds(slot * ROWS + part * PART, PART)]
+        return pltpu.make_async_remote_copy(
+            src_ref=at,
+            dst_ref=at,
+            send_sem=win_send.at[number, part],
+            recv_sem=win_recv.at[slot, part],
+            device_id=device,
+            device_id_type=MESH,
+        )
+
+    def window_copy_to(number, part, slot, slot_there, device):
+        at = window.at[pl.ds(slot * ROWS + part * PART, PART)]
+        there = window.at[pl.ds(slot_there * ROWS + part * PART, PART)]
+        return pltpu.make_async_remote_copy(
+            src_ref=at,
+            dst_ref=there,
+            send_sem=win_send.at[number, part],
+            recv_sem=win_recv.at[slot_there, part],
+            device_id=device,
+            device_id_type=MESH,
+        )
+
+    def window_send(number, part, slot, device, slot_there=None):
+        slot_there = slot if slot_there is None else slot_there
+        copy = window_copy_to(number, part, slot, slot_there, device)
+        copy.start()
+        started.append(copy)
+
+    def window_wait(part, slot):
+        window_copy(0, part, slot, to_sibling).wait_recv()
+
+    for part in range(PARTS):
+        window_send(0, part, 4 + dom, (near_by(1), to_next), dom)
+        window_send(1, part, 4 + dom, (near_by(-1), to_last), 8 + dom)
+    for part in range(PARTS):
+        window_send(2, part, 4 + dom, to_across)
+    for part in range(PARTS):
+        window_send(3, part, 4 + dom, to_sibling)
     lane_row = iota((1, 128), 1)
     row = jnp.zeros((1, 128), F32)
     edge_of_row = iota((EDGES, 128), 0)
@@ -165,76 +254,57 @@
         own_target = jnp.where(edge_of_row == edge, value, own_target)
     for scan in range(SCAN_DEV):
         row = jnp.where(lane_row == EDGES + scan, anchor_ref[scan], row)
-    early_own[0] = row
-    early[pl.ds(REACH * 4 + dom, 1)] = row.reshape(1, 1, 128)
-    early[pl.ds(TILES, PAD - TILES)] = jnp.zeros((PAD - TILES, 1, 128), F32)
+    early[pl.ds(own_slot, 1)] = row.reshape(1, 1, 128)
+    early_copies = halo_push(early, early_send, early_recv)
+    started.append(early_copies)
+    early[pl.ds(TILES, 4)] = jnp.zeros((4, 1, 128), F32)
     for step in range(GN_ITERS):
-        gram[step, pl.ds(TILES, PAD - TILES)] = jnp.zeros((PAD - TILES, 8, 128), F32)
-
-    pl.semaphore_wait(barrier, len(everyone))
-
-    def push(source, at_partner, here, send_sem, recv_sem, partners):
-        copies = []
-        for number, (device, mine, theirs) in enumerate(partners):
-            copy = pltpu.make_async_remote_copy(
-                src_ref=source,
-                dst_ref=at_partner(mine),
-                send_sem=send_sem(number),
-                recv_sem=recv_sem(mine),
-                device_id=device,
-                device_id_type=MESH,
-            )
-            copy.start()
-            arrival = pltpu.make_async_remote_copy(
-                src_ref=source,
-                dst_ref=here(theirs),
-                send_sem=send_sem(number),
-                recv_sem=recv_sem(theirs),
-                device_id=device,
-                device_id_type=MESH,
-            )
-            copies.append((copy, arrival))
-        return copies
-
-    started = []
-    tile_slot = lambda slot: window.at[pl.ds(slot * 32, 32)]
-    window_copies = push(
-        boundary_ref,
-        tile_slot,
-        tile_slot,
-        lambda n: win_send.at[n],
-        lambda n: win_recv.at[n],
-        window_partners,
-    )
-    early_slot = lambda slot: early.at[pl.ds(slot, 1)]
-    early_copies = push(
-        early_own,
-        early_slot,
-        early_slot,
-        lambda n: early_send.at[n],
-        lambda n: early_recv.at[n],
-        halo_partners,
-    )
-    started += window_copies + early_copies
-
-    def gather_scan(scan, carry):
+        gram[step, pl.ds(TILES, 4)] = jnp.zeros((4, 8, 128), F32)
+
+    def gather_scan(scan):
         indices = corr_source_ref[scan].reshape(EDGE_SCAN * CT, 128)
         low = lax.bitwise_and(indices, 127)
         high = lax.shift_right_logical(indices, 7)
-        found = [jnp.zeros((EDGE_SCAN * CT, 128), F32) for _ in range(3)]
-        for block in range(32):
-            here = high == block
-            for comp in range(3):
-                line = source_ref[scan, pl.ds(comp, 1), pl.ds(block * 128, 128)]
-                wide = jnp.broadcast_to(line, (EDGE_SCAN * CT, 128))
-                value = jnp.take_along_axis(wide, low, axis=1, mode="promise_in_bounds")
-                found[comp] = jnp.where(here, value, found[comp])
+
+        def gather_blocks(group, found):
+            found = list(found)
+            for number in range(8):
+                block = group * 8 + number
+                here = high == block
+                for comp in range(3):
+                    at = pl.multiple_of(block * 128, 128)
+                    line = source_ref[comp, pl.ds(scan, 1), pl.ds(at, 128)]
+                    wide = jnp.broadcast_to(line, (EDGE_SCAN * CT, 128))
+                    value = jnp.take_along_axis(wide, low, axis=1, mode="promise_in_bounds")
+                    found[comp] = jnp.where(here, value, found[comp])
+            return tuple(found)
+
+        empty = jnp.zeros((EDGE_SCAN * CT, 128), F32)
+        found = lax.fori_loop(0, 4, gather_blocks, (empty, empty, empty))
         for comp in range(3):
             picked[comp, pl.ds(scan * 16, 16), :] = found[comp]
-        return carry
-
-    lax.fori_loop(0, SCAN_DEV, gather_scan, 0)
-
+
+    loads[1].wait()
+    loads[2].wait()
+    for part in range(PARTS):
+        gather_scan(part)
+        for number, slot in ((4, to_last), (5, 8 + to_next)):
+            window_wait(part, slot)
+            window_send(number, part, slot, to_across)
+            window_send(number + 2, part, slot, to_sibling)
+        window_wait(part, 4 + across)
+        window_send(8, part, 4 + across, to_sibling)
+    gather_scan(2)
+    gather_scan(3)
+    for part in range(PARTS):
+        for number, slot in (
+            (9, lax.bitwise_xor(to_last, 2)),
+            (10, 8 + lax.bitwise_xor(to_next, 2)),
+        ):
+            window_wait(part, slot)
+            window_send(number, part, slot, to_sibling)
+
+    loads[3].wait()
     start = near_by(-REACH) * 16
     first_tile = start // 128
     next_tile = lax.rem(first_tile + 1, groups * 16 // 128)
@@ -274,8 +344,7 @@
     left = to_half == 0
     left_256 = iota((256, 128), 1) < 64
 
-    for _, arrival in early_copies:
-        arrival.wait_recv()
+    early_copies.wait_recv()
     rows = early[...].reshape(PAD, 128)
     rows_turned = jnp.concatenate([rows, jnp.zeros((128 - PAD, 128), F32)], axis=0).T
     lane8 = iota((8, 128), 1)
@@ -301,22 +370,21 @@
     mine = to_lane == EDGES + (node_128 & 3)
     anchor = jnp.sum(jnp.where(mine, anchor_rows, 0.0), axis=1, keepdims=True)
     anchor = jnp.where(node_128 < TILES * 4, jnp.broadcast_to(anchor, (128, 128)), 1.0)
-    own_nodes = (
-        (node_128 // 4 == REACH * 4 + dom)
-        & (to_lane < 6)
-    )
-
-    own_tiles.wait()
-    for _, arrival in window_copies:
-        arrival.wait_recv()
+    own_nodes = (node_128 // 16 == REACH) & (to_lane < 6)
+
+    for part in range(PARTS):
+        for other in (sibling, lax.bitwise_xor(dom, 3)):
+            for offset in range(3):
+                window_wait(part, offset * 4 + other)
+    loads[4].wait()
 
     def gather_edge(edge, carry):
         scan = edge // EDGE_SCAN
         slot = lax.rem(edge, EDGE_SCAN)
-        first = target_ref[scan, slot] * 8
+        first = target_ref[scan, slot] * 48
         lanes = corr_lane_ref[scan, slot]
         for chunk in range(CT):
-            tile = window[first + tile_ref[scan, slot, chunk]]
+            tile = window[pl.ds(first + tile_ref[scan, slot, chunk], 8, stride=8), :]
             spread = jnp.broadcast_to(lanes[chunk : chunk + 1], (8, 128))
             value = jnp.take_along_axis(tile, spread, axis=1, mode="promise_in_bounds")
             chosen[pl.ds(pl.multiple_of(edge * 32 + chunk * 8, 8), 8), :] = value
@@ -381,20 +449,10 @@
                 if a < 6:
                     place = place | (msg_pos == b * 8 + a)
                 message = jnp.where(in_half & place, total, message)
-        gram_own[step, 0] = message
-        gram[step, pl.ds(REACH * 4 + dom, 1)] = message.reshape(1, 8, 128)
-        gram_slot = lambda slot: gram.at[step, pl.ds(slot, 1)]
-        gram_copies = push(
-            gram_own.at[step],
-            gram_slot,
-            gram_slot,
-            lambda n: gram_send.at[step, n],
-            lambda n: gram_recv.at[step, n],
-            halo_partners,
-        )
-        started += gram_copies
-        for _, arrival in gram_copies:
-            arrival.wait_recv()
+        gram[step, pl.ds(own_slot, 1)] = message.reshape(1, 8, 128)
+        gram_copies = halo_push(gram.at[step], gram_send.at[step], gram_recv.at[step])
+        started.append(gram_copies)
+        gram_copies.wait_recv()
         terms = gram[step].reshape(PAD * 8, 128)
 
         def at_nodes(select, value):
@@ -417,14 +475,7 @@
         image = apply_system(scaled)
         second = image * inverse
 
-        own_in = jnp.concatenate(
-            [
-                ends[pl.ds(pl.multiple_of((REACH * 4 + dom) * 8, 8), 8), :],
-                jnp.zeros((8, 256), F32),
-            ],
-            axis=0,
-        ).astype(BF16)
-        own_diff = difference(own_in, second)
+        own_diff = difference(ends_in[REACH * 32 : REACH * 32 + 32], second)
         first_row = as_select(
             (lax.shift_right_logical(from_lane, 6) == to_half)
             & (from_a == 0)
@@ -432,7 +483,7 @@
             & (to_a < 6)
         )
         own_diff_a = pick_right(own_diff, first_row)
-        quad = (message * own_diff[:8]) * own_diff_a[:8]
+        quad = (terms[REACH * 32 : REACH * 32 + 32] * own_diff) * own_diff_a
 
         def inner(a, b):
             return jnp.sum(jnp.where(own_nodes, a * b, 0.0), keepdims=True)
@@ -445,34 +496,26 @@
         for number, value in enumerate((energy, curve, cross, bend)):
             sums_row = jnp.where(lane_row == number, value, sums_row)
 
-        def exchange(value, own, buffer, spot, count, send, recv, partners):
-            own[step, 0] = value
+        def exchange(value, buffer, spot, count, send, recv, partners):
             buffer[step, pl.ds(spot, 1)] = value.reshape(1, 1, 128)
-            slot = lambda n: buffer.at[step, pl.ds(n, 1)]
-            copies = push(
-                own.at[step],
-                slot,
-                slot,
-                lambda n: send.at[step, n],
-                lambda n: recv.at[step, n],
-                partners,
+            own = buffer.at[step, pl.ds(spot, 1)]
+            push(
+                [(own, buffer.at[step, pl.ds(at, 1)], device) for device, at in partners],
+                send.at[step],
+                recv.at[step],
             )
-            for _, arrival in copies:
-                arrival.wait_recv()
-            gathered = buffer[step].reshape(count, 128)
-            return copies, jnp.sum(gathered, axis=0, keepdims=True)
+            others = whole(
+                buffer.at[step, pl.ds(0, count - 1)], send.at[step], recv.at[step]
+            )
+            others.wait_recv()
+            started.append(others)
+            return jnp.sum(buffer[step].reshape(count, 128), axis=0, keepdims=True)
 
         scaled_turned = scaled.T[:8]
         second_turned = second.T[:8]
-        copies, sums_row = exchange(
-            sums_row, near_own, near, sub_high * 4 + dom, 8, near_send, near_recv, near_partners
-        )
-        started += copies
-        copies, sums_row = exchange(
-            sums_row, far_own, far, sub_low, half_groups, far_send, far_recv, far_partners
-        )
-        started += copies
-
+        sums_row = exchange(
+            sums_row, far, sub, groups, far_send, far_recv, sum_partners
+        )
         energy, curve, cross, bend = [sums_row[:, k : k + 1] for k in range(4)]
         step_one = energy / curve
         renewed = step_one * step_one * cross - energy
@@ -508,60 +551,56 @@
 
     final = jnp.concatenate(pose + [jnp.zeros((4, 128), F32)], axis=0)
     final = pltpu.roll(final, 128 - (REACH * 16 + dom * SCAN_DEV), 1)
-    out_ref[...] = final[:12, :SCAN_DEV]
-
-    for copy, _ in started:
+    out_ref[...] = final.T[:SCAN_DEV, :12]
+
+    for copy in started:
         copy.wait_send()
 
 
 def local(groups, source_points, boundary, poses, anchor, edge_target, corr_tile, corr_source, corr_lane):
     vmem = pl.BlockSpec(memory_space=pltpu.VMEM)
     smem = pl.BlockSpec(memory_space=pltpu.SMEM)
+    hbm = pl.BlockSpec(memory_space=pl.ANY)
     dma = pltpu.SemaphoreType.DMA
-    halo = TILES - 1
-    far = groups // 2
     return pl.pallas_call(
         functools.partial(kernel, groups),
-        out_shape=jax.ShapeDtypeStruct((12, SCAN_DEV), F32),
-        in_specs=[vmem, vmem, vmem, smem, smem, smem, vmem, vmem],
+        out_shape=jax.ShapeDtypeStruct((SCAN_DEV, 12), F32),
+        in_specs=[hbm, hbm, hbm, smem, smem, smem, hbm, hbm],
         out_specs=vmem,
         scratch_shapes=[
-            pltpu.VMEM((12 * 32, 8, 128), F32),
+            pltpu.VMEM(corr_source.shape, jnp.int32),
+            pltpu.VMEM(corr_lane.shape, jnp.int32),
+            pltpu.VMEM((3, SCAN_DEV, source_points.shape[2]), F32),
+            pltpu.VMEM(poses.shape, F32),
+            pltpu.VMEM((12 * ROWS + 16, 128), F32),
             pltpu.VMEM((PAD, 1, 128), F32),
-            pltpu.VMEM((1, 1, 128), F32),
             pltpu.VMEM((GN_ITERS, PAD, 8, 128), F32),
-            pltpu.VMEM((GN_ITERS, 1, 8, 128), F32),
-            pltpu.VMEM((GN_ITERS, 8, 1, 128), F32),
-            pltpu.VMEM((GN_ITERS, 1, 1, 128), F32),
-            pltpu.VMEM((GN_ITERS, far, 1, 128), F32),
-            pltpu.VMEM((GN_ITERS, 1, 1, 128), F32),
+            pltpu.VMEM((GN_ITERS, groups, 1, 128), F32),
             pltpu.VMEM((3, 64, 128), F32),
             pltpu.VMEM((512, 128), F32),
             pltpu.VMEM((9, CT, EDGES, 128), F32),
             pltpu.VMEM((PAD * 8, 256), F32),
-            dma((11,)),
-            dma((12,)),
-            dma((halo,)),
-            dma((TILES,)),
-            dma((GN_ITERS, halo)),
-            dma((GN_ITERS, TILES)),
-            dma((GN_ITERS, 7)),
-            dma((GN_ITERS, 8)),
-            dma((GN_ITERS, far - 1)),
-            dma((GN_ITERS, far)),
+            dma((11, PARTS)),
+            dma((12, PARTS)),
             dma,
+            dma,
+            dma((GN_ITERS,)),
+            dma((GN_ITERS,)),
+            dma((GN_ITERS,)),
+            dma((GN_ITERS,)),
+            dma((5,)),
         ],
         compiler_params=pltpu.CompilerParams(collective_id=0, has_side_effects=True),
     )(
-        source_points,
-        jnp.pad(boundary.reshape(32, 6, 128), ((0, 0), (0, 2), (0, 0))),
+        source_points.transpose(1, 0, 2),
+        boundary.transpose(0, 2, 1, 3).reshape(ROWS, 128),
         poses,
         anchor,
         edge_target,
         corr_tile,
         corr_source,
         corr_lane,
-    )
+    ).T
 
 
 def solution(mesh):

time: 77.1 us -> 59.8 us (0.78)
  Pallas kernels: 73.1 us -> 58.3 us
  local copies, waits for them, and re-layouts: 3.81 us -> 1.26 us
    pallas_call x1, Pallas kernels: 73.1 us -> 58.3 us  [local(): pl.pallas_call(functools.partial(kernel, groups), out_shape=jax.ShapeDtyp...]
    pallas_call x1 -> x0, local copies, waits for them, and re-layouts: 1.35 us -> none  [local(): pl.pallas_call(functools.partial(kernel, groups), out_shape=jax.ShapeDtyp...]
    unnamed x4 -> x1, local copies, waits for them, and re-layouts: 1.79 us -> 1.26 us
where the time goes in v2:
time: 59.8 us; the launch traced here: 59.6 us
  Pallas kernels  58.3 us (97%)
  local copies, waits for them, and re-layouts  1.26 us (2%)
    pallas_call x1, Pallas kernels, local(): pl.pallas_call(functools.partial(kernel, groups), out_shape=jax.ShapeDtyp...  58.3 us
    unnamed x1, local copies, waits for them, and re-layouts  1.26 us

profile of v2, /device:TPU:1, one launch (start us, length us, event | category | flops | bytes accessed | tf_op | source)
XLA Modules:
  0.0 59.6 jit_solution(13580891902717309247)
XLA Ops:
  0.0 58.3 %shard_map.82 = f32[4,12]{1,0:T(4,128)} custom-call(f32[3,4,4096]{2,1,0:T(4,128)} %bitcast.5, f32[192,128]{1,0:T(8,128)} %bitcast.6, f32[12,1024]{1,0:T(8,128)} %poses_hbm.1, f32[4]{0:T(128)} %anchor_ref.1, s32[4,4]{1,0:T(4,128)} %target_ref.1, s32[4,4,4]{2,1,0:T(4,128)} %tile_ref.1, s32[4,4,4,128]{3,2,1,0:T(4,128)} %corr_source_hbm.1, ...), custom_call_target="tpu_custom_call" | custom-call | tf_op jit(solution)/shard_map/pallas_call | solution.py:565
  58.3 1.3 %copy.10 = f32[12,4]{0,1:T(4,128)} copy(f32[12,4]{0,1:T(4,128)} %bitcast.7) | data formatting | bytes 384

commit v3 on v2

--- a/solution.py
+++ b/solution.py
@@ -30,12 +30,12 @@
     return lax.broadcasted_iota(jnp.int32, shape, dim)
 
 
-def parts_of(value):
-    first = value.astype(BF16)
-    rest = value - first.astype(F32)
-    second = rest.astype(BF16)
-    third = (rest - second.astype(F32)).astype(BF16)
-    return (third, second, first)
+def parts_of(value, count=2):
+    parts = []
+    for _ in range(count):
+        parts.append(value.astype(BF16))
+        value = value - parts[-1].astype(F32)
+    return parts[::-1]
 
 
 def dot(a, b):
@@ -43,20 +43,20 @@
 
 
 def pick_left(select, value):
-    third, second, first = parts_of(value)
-    return (dot(select, third) + dot(select, second)) + dot(select, first)
+    second, first = parts_of(value)
+    return dot(select, second) + dot(select, first)
 
 
 def pick_right(value, select):
-    third, second, first = parts_of(value)
-    return (dot(third, select) + dot(second, select)) + dot(first, select)
+    second, first = parts_of(value)
+    return dot(second, select) + dot(first, select)
 
 
 def pick_turned(select, value):
     turned = (((1,), (1,)), ((), ()))
     third, second, first = [
         lax.dot_general(select, part, turned, preferred_element_type=F32)
-        for part in parts_of(value)
+        for part in parts_of(value, 3)
     ]
     return (third + second) + first
 
@@ -111,6 +111,7 @@
     far_send,
     far_recv,
     load_sem,
+    word,
 ):
     sub = lax.axis_index("sub")
     dom = lax.axis_index("dom")
@@ -123,7 +124,7 @@
 
     halo_partners = [
         ((near_by(offset), lax.bitwise_xor(dom, other)), (REACH - offset) * 4 + dom)
-        for distance in range(REACH + 1)
+        for distance in range(REACH, -1, -1)
         for offset in ((distance, -distance) if distance else (0,))
         for other in range(4)
         if distance or other
@@ -157,11 +158,30 @@
     for load in loads:
         load.start()
     barrier = pltpu.get_barrier_semaphore()
-    everyone = halo_partners + sum_partners
-    for device, _ in everyone:
-        pl.semaphore_signal(barrier, inc=1, device_id=device, device_id_type=MESH)
-
-    pl.semaphore_wait(barrier, len(everyone))
+    z_size = groups // 8
+    z_spot = lax.rem(sub, z_size)
+    y_spot = lax.rem(sub // z_size, 4)
+    z_line = [
+        (sub - z_spot + lax.rem(z_spot + turn, z_size), dom) for turn in range(1, z_size)
+    ]
+    y_line = [
+        (
+            sub_high * half_groups + lax.rem(y_spot + turn, 4) * z_size + z_spot,
+            dom,
+        )
+        for turn in range(1, 4)
+    ]
+    x_line = [((1 - sub_high) * half_groups + sub_low, lax.bitwise_xor(dom, 2))]
+
+    def signal_all(semaphore, devices):
+        for device in devices:
+            pl.semaphore_signal(semaphore, inc=1, device_id=device, device_id_type=MESH)
+
+    greeted = [device for device, _ in halo_partners] + z_line + y_line + x_line
+    signal_all(barrier, greeted)
+
+    pl.semaphore_wait(barrier, len(greeted))
+    started = []
 
     def push(copies, send_sem, recv_sem):
         for source, target, device in copies:
@@ -195,7 +215,6 @@
         )
         return whole(buffer.at[pl.ds(0, TILES - 1)], send, recv)
 
-    started = []
     loads[0].wait()
     sibling = lax.bitwise_xor(dom, 1)
     across = lax.bitwise_xor(dom, 2)
@@ -256,6 +275,7 @@
         row = jnp.where(lane_row == EDGES + scan, anchor_ref[scan], row)
     early[pl.ds(own_slot, 1)] = row.reshape(1, 1, 128)
     early_copies = halo_push(early, early_send, early_recv)
+    signal_all(word.at[0], y_line)
     started.append(early_copies)
     early[pl.ds(TILES, 4)] = jnp.zeros((4, 1, 128), F32)
     for step in range(GN_ITERS):
@@ -294,6 +314,8 @@
             window_send(number + 2, part, slot, to_sibling)
         window_wait(part, 4 + across)
         window_send(8, part, 4 + across, to_sibling)
+    pl.semaphore_wait(word.at[0], len(y_line))
+    signal_all(word.at[1], x_line)
     gather_scan(2)
     gather_scan(3)
     for part in range(PARTS):
@@ -376,6 +398,7 @@
         for other in (sibling, lax.bitwise_xor(dom, 3)):
             for offset in range(3):
                 window_wait(part, offset * 4 + other)
+    pl.semaphore_wait(word.at[1], len(x_line))
     loads[4].wait()
 
     def gather_edge(edge, carry):
@@ -390,7 +413,7 @@
             chosen[pl.ds(pl.multiple_of(edge * 32 + chunk * 8, 8), 8), :] = value
         return carry
 
-    lax.fori_loop(0, EDGES, gather_edge, 0)
+    lax.fori_loop(0, EDGES, gather_edge, 0, unroll=True)
     for chunk in range(CT):
         for comp in range(3):
             comps[comp, chunk] = picked[comp, pl.ds(chunk, EDGES, stride=CT), :]
@@ -564,7 +587,7 @@
     dma = pltpu.SemaphoreType.DMA
     return pl.pallas_call(
         functools.partial(kernel, groups),
-        out_shape=jax.ShapeDtypeStruct((SCAN_DEV, 12), F32),
+        out_shape=pltpu.VMEM((SCAN_DEV, 12), F32),
         in_specs=[hbm, hbm, hbm, smem, smem, smem, hbm, hbm],
         out_specs=vmem,
         scratch_shapes=[
@@ -589,6 +612,7 @@
             dma((GN_ITERS,)),
             dma((GN_ITERS,)),
             dma((5,)),
+            pltpu.SemaphoreType.REGULAR((2,)),
         ],
         compiler_params=pltpu.CompilerParams(collective_id=0, has_side_effects=True),
     )(

time: 59.8 us -> 54.7 us (0.915)
  Pallas kernels: 58.3 us -> 54 us
  local copies, waits for them, and re-layouts: 1.26 us -> 0.58 us
    pallas_call x1, Pallas kernels: 58.3 us -> 54 us  [local(): pl.pallas_call(functools.partial(kernel, groups), out_shape=pltpu.VMEM((S...]
    unnamed x1, local copies, waits for them, and re-layouts: 1.26 us -> 0.58 us
where the time goes in v3:
time: 54.7 us; the launch traced here: 54.5 us
  Pallas kernels  54 us (99%)
  local copies, waits for them, and re-layouts  0.58 us (1%)
    pallas_call x1, Pallas kernels, local(): pl.pallas_call(functools.partial(kernel, groups), out_shape=pltpu.VMEM((S...  54 us

profile of v3, /device:TPU:1, one launch (start us, length us, event | category | flops | bytes accessed | tf_op | source)
XLA Modules:
  0.0 54.5 jit_solution(10438915517358237699)
XLA Ops:
  0.0 54.0 %shard_map.82 = f32[4,12]{1,0:T(4,128)S(1)} custom-call(f32[3,4,4096]{2,1,0:T(4,128)} %bitcast.6, f32[192,128]{1,0:T(8,128)} %bitcast.7, f32[12,1024]{1,0:T(8,128)} %poses_hbm.1, f32[4]{0:T(128)} %anchor_ref.1, s32[4,4]{1,0:T(4,128)} %target_ref.1, s32[4,4,4]{2,1,0:T(4,128)} %tile_ref.1, s32[4,4,4,128]{3,2,1,0:T(4,128)} %corr_source_hbm.1, ...), custom_call_target="tpu_custom_call" | custom-call | tf_op jit(solution)/shard_map/pallas_call | solution.py:588
  54.0 0.6 %copy.10 = f32[12,4]{0,1:T(4,128)} copy(f32[12,4]{0,1:T(4,128)S(1)} %bitcast.5) | data formatting | bytes 384

commit v4 on v3

--- a/solution.py
+++ b/solution.py
@@ -42,14 +42,25 @@
     return jnp.dot(a, b, preferred_element_type=F32)
 
 
-def pick_left(select, value):
-    second, first = parts_of(value)
-    return dot(select, second) + dot(select, first)
-
-
-def pick_right(value, select):
-    second, first = parts_of(value)
-    return dot(second, select) + dot(first, select)
+def rows_times(value, select):
+    stacked = jnp.concatenate([part.astype(F32) for part in parts_of(value, 3)], axis=0)
+    product = dot(stacked.astype(BF16), select)
+    return (product[0:8] + product[8:16]) + product[16:24]
+
+
+def regroup(tiles):
+    group = lax.shift_right_logical(iota((8, 128), 1), 4)
+    for bit in range(3):
+        size = 1 << bit
+        low = lax.bitwise_and(group, size) == 0
+        tiles = list(tiles)
+        for first in range(8):
+            if first & size:
+                continue
+            one, two = tiles[first], tiles[first + size]
+            tiles[first] = jnp.where(low, one, pltpu.roll(two, size * 16, 1))
+            tiles[first + size] = jnp.where(low, pltpu.roll(one, 128 - size * 16, 1), two)
+    return tiles
 
 
 def pick_turned(select, value):
@@ -351,20 +362,8 @@
         axis=0,
     ).astype(BF16)
 
-    from_lane = iota((128, 128), 0)
-    to_lane = iota((128, 128), 1)
-    from_a = lax.shift_right_logical(from_lane, 3) & 7
-    from_b = from_lane & 7
-    to_half = lax.shift_right_logical(to_lane, 6)
-    to_a = lax.shift_right_logical(to_lane, 3) & 7
-    to_b = to_lane & 7
-    used = (to_a < 6) & (to_b < 6) & (from_b < 6)
-    as_select = lambda mask: mask.astype(F32).astype(BF16)
-    over_b = as_select(used & (from_a == to_b))
-    slopes_out = as_select(used & (from_a == 6) & (from_b == to_b))
-    diagonal_out = as_select(used & (from_a == from_b) & (from_b == to_b))
-    left = to_half == 0
-    left_256 = iota((256, 128), 1) < 64
+    row_of = iota((16, 6 * 128), 0) == lax.shift_right_logical(iota((16, 6 * 128), 1), 7)
+    into_rows = jnp.where(row_of, 1.0, 0.0).astype(BF16)
 
     early_copies.wait_recv()
     rows = early[...].reshape(PAD, 128)
@@ -372,27 +371,28 @@
     lane8 = iota((8, 128), 1)
     row8 = iota((8, 128), 0)
     for tile in range(TILES):
-        for half in range(2):
-            target = rows_turned[half * 8 : half * 8 + 8, tile : tile + 1]
-            target_lane = target + float((tile // 4 - 1) * 16)
-            source_lane = tile * 4 + half * 2 + row8 // 4
-            ends[pl.ds(tile * 8, 8), pl.ds(half * 128, 128)] = (
-                lane8 == source_lane
-            ).astype(F32) - (lane8.astype(F32) == target_lane).astype(F32)
-    ends[pl.ds(TILES * 8, (PAD - TILES) * 8), :] = jnp.zeros(((PAD - TILES) * 8, 256), F32)
+        target = rows_turned[:EDGES, tile : tile + 1]
+        target_lane = target + float((tile // 4 - 1) * 16)
+        source_lane = tile * 4 + edge_of_row // EDGE_SCAN
+        ends[pl.ds(tile * EDGES, EDGES), :] = (lane16 == source_lane).astype(F32) - (
+            lane16.astype(F32) == target_lane
+        ).astype(F32)
+    ends[pl.ds(TILES * EDGES, (PAD - TILES) * EDGES), :] = jnp.zeros(
+        ((PAD - TILES) * EDGES, 128), F32
+    )
     ends_f32 = ends[...]
-    ends_turned_f32 = ends_f32.T
-    ends_in = ends_f32.astype(BF16)
-    ends_out = ends_turned_f32.astype(BF16)
-    ends_abs = jnp.abs(ends_turned_f32).astype(BF16)
-    node = iota((128, PAD), 0)
-    of_tile = as_select(node // 4 == iota((128, PAD), 1))
-    anchor_rows = pick_left(of_tile, rows)
-    node_128 = from_lane
-    mine = to_lane == EDGES + (node_128 & 3)
-    anchor = jnp.sum(jnp.where(mine, anchor_rows, 0.0), axis=1, keepdims=True)
-    anchor = jnp.where(node_128 < TILES * 4, jnp.broadcast_to(anchor, (128, 128)), 1.0)
-    own_nodes = (node_128 // 16 == REACH) & (to_lane < 6)
+    ends_out = ends_f32.astype(BF16)
+    ends_abs = jnp.abs(ends_f32).astype(BF16)
+    ends_in = ends_f32.T.astype(BF16)
+    of_tile = jnp.where(iota((128, 128), 0) == iota((128, 128), 1) // 4, 1.0, 0.0).astype(BF16)
+    anchor_rows = rows_times(rows_turned[EDGES : EDGES + 8], of_tile)
+    anchor = jnp.sum(
+        jnp.where(row8 == lax.bitwise_and(lane8, 3), anchor_rows, 0.0), axis=0, keepdims=True
+    )
+    anchor = jnp.broadcast_to(anchor, (8, 128))
+    anchor = jnp.where(lane8 < TILES * 4, anchor, 1.0)
+    own_nodes = (lane8 // 16 == REACH) & (row8 < 6)
+    own_edges = (lane8 >= 64) & (row8 < 6)
 
     for part in range(PARTS):
         for other in (sibling, lax.bitwise_xor(dom, 3)):
@@ -420,101 +420,99 @@
         for comp in range(6):
             comps[3 + comp, chunk] = chosen[pl.ds(chunk * 8 + comp, EDGES, stride=32), :]
 
-    msg_pos = lane8 & 63
 
     for step in range(GN_ITERS):
         pose_rows = jnp.concatenate(pose + [jnp.zeros((4, 128), F32)], axis=0)
         pose_ends = pick_turned(own_ends, pose_rows)
-        message = jnp.zeros((8, 128), F32)
-        for half in range(2):
-            here = [
-                jnp.broadcast_to(pose_ends[half * 8 : half * 8 + 8, k : k + 1], (8, 128))
-                for k in range(12)
-            ]
-            there = [
-                jnp.broadcast_to(
-                    pose_ends[EDGES + half * 8 : EDGES + half * 8 + 8, k : k + 1], (8, 128)
-                )
-                for k in range(12)
-            ]
-            sums = {}
-            for chunk in range(CT):
-                data = [comps[k, chunk, pl.ds(half * 8, 8), :] for k in range(9)]
-
-                def turn(matrix, vector):
-                    return [
-                        matrix[3 * i] * vector[0]
-                        + matrix[3 * i + 1] * vector[1]
-                        + matrix[3 * i + 2] * vector[2]
-                        for i in range(3)
-                    ]
-
-                placed = [v + t for v, t in zip(turn(here[:9], data[0:3]), here[9:])]
-                target = [v + t for v, t in zip(turn(there[:9], data[3:6]), there[9:])]
-                normal = turn(there[:9], data[6:9])
-                offset = [q - p for q, p in zip(target, placed)]
-                misfit = normal[0] * offset[0] + normal[1] * offset[1] + normal[2] * offset[2]
-                jac = [
-                    placed[1] * normal[2] - placed[2] * normal[1],
-                    placed[2] * normal[0] - placed[0] * normal[2],
-                    placed[0] * normal[1] - placed[1] * normal[0],
-                ] + normal
-                for a, b in PAIRS:
-                    term = jac[a] * jac[b]
-                    sums[a, b] = sums[a, b] + term if chunk else term
-                for b in range(6):
-                    term = jac[b] * misfit
-                    sums[6, b] = sums[6, b] + term if chunk else term
-            in_half = lane8 // 64 == half
-            for (a, b), value in sums.items():
-                total = jnp.sum(value, axis=1, keepdims=True) * (1.0 / SAMPLES)
-                place = msg_pos == a * 8 + b
-                if a < 6:
-                    place = place | (msg_pos == b * 8 + a)
-                message = jnp.where(in_half & place, total, message)
+        here = [
+            jnp.broadcast_to(pose_ends[:EDGES, k : k + 1], (EDGES, 128)) for k in range(12)
+        ]
+        there = [
+            jnp.broadcast_to(pose_ends[EDGES:, k : k + 1], (EDGES, 128)) for k in range(12)
+        ]
+        sums = {}
+        for chunk in range(CT):
+            data = [comps[k, chunk] for k in range(9)]
+
+            def turn(matrix, vector):
+                return [
+                    matrix[3 * i] * vector[0]
+                    + matrix[3 * i + 1] * vector[1]
+                    + matrix[3 * i + 2] * vector[2]
+                    for i in range(3)
+                ]
+
+            placed = [v + t for v, t in zip(turn(here[:9], data[0:3]), here[9:])]
+            target = [v + t for v, t in zip(turn(there[:9], data[3:6]), there[9:])]
+            normal = turn(there[:9], data[6:9])
+            offset = [q - p for q, p in zip(target, placed)]
+            misfit = normal[0] * offset[0] + normal[1] * offset[1] + normal[2] * offset[2]
+            jac = [
+                placed[1] * normal[2] - placed[2] * normal[1],
+                placed[2] * normal[0] - placed[0] * normal[2],
+                placed[0] * normal[1] - placed[1] * normal[0],
+            ] + normal
+            for a, b in PAIRS:
+                term = jac[a] * jac[b]
+                sums[a, b] = sums[a, b] + term if chunk else term
+            for a in range(6):
+                term = jac[a] * misfit
+                sums[a, 6] = sums[a, 6] + term if chunk else term
+        nothing = jnp.zeros((EDGES, 128), F32)
+        message = None
+        split = {key: parts_of(value) for key, value in sums.items()}
+        for part in range(2):
+            spread = jnp.concatenate(
+                [
+                    jnp.concatenate(
+                        [split[min(a, b), max(a, b)][part] for b in range(7)]
+                        + [nothing.astype(BF16)],
+                        axis=0,
+                    )
+                    for a in range(6)
+                ],
+                axis=1,
+            )
+            term = lax.dot_general(
+                into_rows, spread, (((1,), (1,)), ((), ())), preferred_element_type=F32
+            )
+            message = term if message is None else message + term
+        message = message[:8] * (1.0 / SAMPLES)
         gram[step, pl.ds(own_slot, 1)] = message.reshape(1, 8, 128)
         gram_copies = halo_push(gram.at[step], gram_send.at[step], gram_recv.at[step])
         started.append(gram_copies)
         gram_copies.wait_recv()
-        terms = gram[step].reshape(PAD * 8, 128)
-
-        def at_nodes(select, value):
-            both = pick_left(select, value)
-            return jnp.where(left, both[:128], both[128:])
-
-        def difference(select, value):
-            twice = jnp.concatenate([value, value], axis=0)
-            sides = iota((256, 128), 0) < 128
-            return pick_left(select, jnp.where(sides == left_256, twice, 0.0))
-
-        def apply_system(value):
-            image = at_nodes(ends_out, terms * difference(ends_in, value))
-            return pick_right(image, over_b) + anchor * value
-
-        residual = pick_right(at_nodes(ends_out, terms), slopes_out)
-        diagonal = pick_right(at_nodes(ends_abs, terms), diagonal_out) + anchor
+        tiles = gram[step]
+        grouped = [regroup([tiles[8 * g + t] for t in range(8)]) for g in range(PAD // 8)]
+        blocks = [
+            jnp.concatenate([group[b] for group in grouped], axis=1) for b in range(7)
+        ]
+        diagonal_terms = jnp.zeros((8, PAD * EDGES), F32)
+        row_all = iota((8, PAD * EDGES), 0)
+        for b in range(6):
+            diagonal_terms = jnp.where(row_all == b, blocks[b], diagonal_terms)
+        residual = rows_times(blocks[6], ends_out)
+        diagonal = rows_times(diagonal_terms, ends_abs) + anchor
         inverse = 1.0 / diagonal
         scaled = residual * inverse
-        image = apply_system(scaled)
+        spread = rows_times(scaled, ends_in)
+        pushed = blocks[0] * spread[0:1]
+        for b in range(1, 6):
+            pushed = pushed + blocks[b] * spread[b : b + 1]
+        image = rows_times(pushed, ends_out) + anchor * scaled
         second = image * inverse
-
-        own_diff = difference(ends_in[REACH * 32 : REACH * 32 + 32], second)
-        first_row = as_select(
-            (lax.shift_right_logical(from_lane, 6) == to_half)
-            & (from_a == 0)
-            & (from_b == to_a)
-            & (to_a < 6)
-        )
-        own_diff_a = pick_right(own_diff, first_row)
-        quad = (terms[REACH * 32 : REACH * 32 + 32] * own_diff) * own_diff_a
-
-        def inner(a, b):
-            return jnp.sum(jnp.where(own_nodes, a * b, 0.0), keepdims=True)
+        own_diff = rows_times(second, ends_in[:, 128:256])
+        own_pushed = grouped[1][0] * own_diff[0:1]
+        for b in range(1, 6):
+            own_pushed = own_pushed + grouped[1][b] * own_diff[b : b + 1]
+
+        def inner(a, b, mask=own_nodes):
+            return jnp.sum(jnp.where(mask, a * b, 0.0), keepdims=True)
 
         energy = inner(residual, scaled)
         curve = inner(scaled, image)
         cross = inner(second, image)
-        bend = inner(anchor * second, second) + jnp.sum(quad, keepdims=True)
+        bend = inner(anchor * second, second) + inner(own_pushed, own_diff, own_edges)
         sums_row = jnp.zeros((1, 128), F32)
         for number, value in enumerate((energy, curve, cross, bend)):
             sums_row = jnp.where(lane_row == number, value, sums_row)
@@ -534,8 +532,6 @@
             started.append(others)
             return jnp.sum(buffer[step].reshape(count, 128), axis=0, keepdims=True)
 
-        scaled_turned = scaled.T[:8]
-        second_turned = second.T[:8]
         sums_row = exchange(
             sums_row, far, sub, groups, far_send, far_recv, sum_partners
         )
@@ -551,9 +547,9 @@
             + ratio * ratio * curve
         )
         step_two = renewed / curve_two
-        increment = (step_one + step_two * (1.0 + ratio)) * scaled_turned - (
+        increment = (step_one + step_two * (1.0 + ratio)) * scaled - (
             step_two * step_one
-        ) * second_turned
+        ) * second
         inc = [increment[k : k + 1] for k in range(6)]
         turn_mat = cayley(0.5 * inc[0], 0.5 * inc[1], 0.5 * inc[2])
         rotated = [
@@ -602,7 +598,7 @@
             pltpu.VMEM((3, 64, 128), F32),
             pltpu.VMEM((512, 128), F32),
             pltpu.VMEM((9, CT, EDGES, 128), F32),
-            pltpu.VMEM((PAD * 8, 256), F32),
+            pltpu.VMEM((PAD * EDGES, 128), F32),
             dma((11, PARTS)),
             dma((12, PARTS)),
             dma,

time: 54.7 us -> 54 us (0.987)
  Pallas kernels: 54 us -> 53.3 us
    pallas_call x1, Pallas kernels: 54 us -> 53.3 us  [local(): pl.pallas_call(functools.partial(kernel, groups), out_shape=pltpu.VMEM((S...]
where the time goes in v4:
time: 54 us; the launch traced here: 53.9 us
  Pallas kernels  53.3 us (99%)
  local copies, waits for them, and re-layouts  0.58 us (1%)
    pallas_call x1, Pallas kernels, local(): pl.pallas_call(functools.partial(kernel, groups), out_shape=pltpu.VMEM((S...  53.3 us

profile of v4, /device:TPU:1, one launch (start us, length us, event | category | flops | bytes accessed | tf_op | source)
XLA Modules:
  0.0 53.9 jit_solution(3408243857277856104)
XLA Ops:
  0.0 53.3 %shard_map.82 = f32[4,12]{1,0:T(4,128)S(1)} custom-call(f32[3,4,4096]{2,1,0:T(4,128)} %bitcast.6, f32[192,128]{1,0:T(8,128)} %bitcast.7, f32[12,1024]{1,0:T(8,128)} %poses_hbm.1, f32[4]{0:T(128)} %anchor_ref.1, s32[4,4]{1,0:T(4,128)} %target_ref.1, s32[4,4,4]{2,1,0:T(4,128)} %tile_ref.1, s32[4,4,4,128]{3,2,1,0:T(4,128)} %corr_source_hbm.1, ...), custom_call_target="tpu_custom_call" | custom-call | tf_op jit(solution)/shard_map/pallas_call | solution.py:584
  53.3 0.6 %copy.10 = f32[12,4]{0,1:T(4,128)} copy(f32[12,4]{0,1:T(4,128)S(1)} %bitcast.5) | data formatting | bytes 384

commit v5 on v4

--- a/solution.py
+++ b/solution.py
@@ -140,19 +140,28 @@
         for other in range(4)
         if distance or other
     ]
-    sum_partners = [
-        ((sub_high * half_groups + lax.rem(sub_low + turn, half_groups), dom), sub)
-        for turn in range(1, half_groups)
-    ] + [
-        (
-            (
-                (1 - sub_high) * half_groups + lax.rem(sub_low + turn, half_groups),
-                lax.bitwise_xor(dom, 2),
-            ),
-            sub,
-        )
-        for turn in range(half_groups)
+    z_size = groups // 8
+    z_spot = lax.rem(sub, z_size)
+    y_spot = lax.rem(sub // z_size, 4)
+
+    def hops(step, size):
+        return min(step, size - step)
+
+    moves = [
+        (x_step, y_step, z_step)
+        for x_step in range(2)
+        for y_step in range(4)
+        for z_step in range(z_size)
+        if x_step or y_step or z_step
     ]
+    moves.sort(key=lambda move: -(move[0] + hops(move[1], 4) + hops(move[2], z_size)))
+    sum_partners = []
+    for x_step, y_step, z_step in moves:
+        half = 1 - sub_high if x_step else sub_high
+        y_there = lax.rem(y_spot + y_step, 4)
+        z_there = lax.rem(z_spot + z_step, z_size)
+        place = half * half_groups + y_there * z_size + z_there
+        sum_partners.append(((place, lax.bitwise_xor(dom, 2 * x_step)), sub))
 
     loads = [
         pltpu.make_async_copy(source, target, load_sem.at[number])
@@ -169,9 +178,6 @@
     for load in loads:
         load.start()
     barrier = pltpu.get_barrier_semaphore()
-    z_size = groups // 8
-    z_spot = lax.rem(sub, z_size)
-    y_spot = lax.rem(sub // z_size, 4)
     z_line = [
         (sub - z_spot + lax.rem(z_spot + turn, z_size), dom) for turn in range(1, z_size)
     ]
@@ -217,14 +223,12 @@
 
     own_slot = REACH * 4 + dom
 
-    def halo_push(buffer, send, recv):
-        own = buffer.at[pl.ds(own_slot, 1)]
+    def halo_push(buffer, rows, send, recv):
+        at = lambda slot, count=1: buffer.at[pl.ds(slot, count), pl.ds(0, rows)]
         push(
-            [(own, buffer.at[pl.ds(slot, 1)], device) for device, slot in halo_partners],
-            send,
-            recv,
-        )
-        return whole(buffer.at[pl.ds(0, TILES - 1)], send, recv)
+            [(at(own_slot), at(slot), device) for device, slot in halo_partners], send, recv
+        )
+        return whole(at(0, TILES - 1), send, recv)
 
     loads[0].wait()
     sibling = lax.bitwise_xor(dom, 1)
@@ -285,12 +289,13 @@
     for scan in range(SCAN_DEV):
         row = jnp.where(lane_row == EDGES + scan, anchor_ref[scan], row)
     early[pl.ds(own_slot, 1)] = row.reshape(1, 1, 128)
-    early_copies = halo_push(early, early_send, early_recv)
+    early_copies = halo_push(early, 1, early_send, early_recv)
     signal_all(word.at[0], y_line)
     started.append(early_copies)
     early[pl.ds(TILES, 4)] = jnp.zeros((4, 1, 128), F32)
     for step in range(GN_ITERS):
         gram[step, pl.ds(TILES, 4)] = jnp.zeros((4, 8, 128), F32)
+        gram[step, pl.ds(0, TILES), pl.ds(6, 2)] = jnp.zeros((TILES, 2, 128), F32)
 
     def gather_scan(scan):
         indices = corr_source_ref[scan].reshape(EDGE_SCAN * CT, 128)
@@ -383,7 +388,26 @@
     ends_f32 = ends[...]
     ends_out = ends_f32.astype(BF16)
     ends_abs = jnp.abs(ends_f32).astype(BF16)
-    ends_in = ends_f32.T.astype(BF16)
+    node_of = iota((128, PAD * EDGES), 0)
+    ends_turned = ends_f32.T
+    far_end = jnp.sum(
+        jnp.where(ends_turned < 0.0, node_of, 0), axis=0, keepdims=True
+    )
+    near_lanes = []
+    far_lanes = []
+    for group in range(PAD // 8):
+        near_lanes.append(group * 32 + lane8 // EDGE_SCAN)
+        far_lanes.append(
+            jnp.broadcast_to(far_end[:, group * 128 : group * 128 + 128], (8, 128))
+        )
+
+    def along_edges(value, group):
+        near = jnp.take_along_axis(value, near_lanes[group], axis=1, mode="promise_in_bounds")
+        far_value = jnp.take_along_axis(
+            value, far_lanes[group], axis=1, mode="promise_in_bounds"
+        )
+        return near - far_value
+
     of_tile = jnp.where(iota((128, 128), 0) == iota((128, 128), 1) // 4, 1.0, 0.0).astype(BF16)
     anchor_rows = rows_times(rows_turned[EDGES : EDGES + 8], of_tile)
     anchor = jnp.sum(
@@ -391,9 +415,6 @@
     )
     anchor = jnp.broadcast_to(anchor, (8, 128))
     anchor = jnp.where(lane8 < TILES * 4, anchor, 1.0)
-    own_nodes = (lane8 // 16 == REACH) & (row8 < 6)
-    own_edges = (lane8 >= 64) & (row8 < 6)
-
     for part in range(PARTS):
         for other in (sibling, lax.bitwise_xor(dom, 3)):
             for offset in range(3):
@@ -479,7 +500,7 @@
             message = term if message is None else message + term
         message = message[:8] * (1.0 / SAMPLES)
         gram[step, pl.ds(own_slot, 1)] = message.reshape(1, 8, 128)
-        gram_copies = halo_push(gram.at[step], gram_send.at[step], gram_recv.at[step])
+        gram_copies = halo_push(gram.at[step], 6, gram_send.at[step], gram_recv.at[step])
         started.append(gram_copies)
         gram_copies.wait_recv()
         tiles = gram[step]
@@ -495,27 +516,34 @@
         diagonal = rows_times(diagonal_terms, ends_abs) + anchor
         inverse = 1.0 / diagonal
         scaled = residual * inverse
-        spread = rows_times(scaled, ends_in)
-        pushed = blocks[0] * spread[0:1]
-        for b in range(1, 6):
-            pushed = pushed + blocks[b] * spread[b : b + 1]
+
+        def push_edges(group, difference):
+            pushed = grouped[group][0] * difference[0:1]
+            for b in range(1, 6):
+                pushed = pushed + grouped[group][b] * difference[b : b + 1]
+            return pushed
+
+        pushed = jnp.concatenate(
+            [push_edges(group, along_edges(scaled, group)) for group in range(PAD // 8)],
+            axis=1,
+        )
         image = rows_times(pushed, ends_out) + anchor * scaled
         second = image * inverse
-        own_diff = rows_times(second, ends_in[:, 128:256])
-        own_pushed = grouped[1][0] * own_diff[0:1]
-        for b in range(1, 6):
-            own_pushed = own_pushed + grouped[1][b] * own_diff[b : b + 1]
-
-        def inner(a, b, mask=own_nodes):
-            return jnp.sum(jnp.where(mask, a * b, 0.0), keepdims=True)
-
-        energy = inner(residual, scaled)
-        curve = inner(scaled, image)
-        cross = inner(second, image)
-        bend = inner(anchor * second, second) + inner(own_pushed, own_diff, own_edges)
-        sums_row = jnp.zeros((1, 128), F32)
-        for number, value in enumerate((energy, curve, cross, bend)):
-            sums_row = jnp.where(lane_row == number, value, sums_row)
+        own_diff = along_edges(second, 1)
+        own_pushed = push_edges(1, own_diff)
+
+        own = slice(REACH * 16, REACH * 16 + 16)
+        packed = jnp.concatenate(
+            [
+                (residual * scaled)[:, own],
+                (scaled * image)[:, own],
+                (second * image)[:, own],
+                (anchor * second * second)[:, own],
+                (own_pushed * own_diff)[:, 64:],
+            ],
+            axis=1,
+        )
+        sums_row = jnp.sum(jnp.where(row8 < 6, packed, 0.0), axis=0, keepdims=True)
 
         def exchange(value, buffer, spot, count, send, recv, partners):
             buffer[step, pl.ds(spot, 1)] = value.reshape(1, 1, 128)
@@ -535,7 +563,11 @@
         sums_row = exchange(
             sums_row, far, sub, groups, far_send, far_recv, sum_partners
         )
-        energy, curve, cross, bend = [sums_row[:, k : k + 1] for k in range(4)]
+        part_of = jnp.minimum(lane_row // 16, 3)
+        energy, curve, cross, bend = [
+            jnp.sum(jnp.where(part_of == k, sums_row, 0.0), axis=1, keepdims=True)
+            for k in range(4)
+        ]
         step_one = energy / curve
         renewed = step_one * step_one * cross - energy
         ratio = renewed / energy

time: 54 us -> 52.2 us (0.967)
  Pallas kernels: 53.3 us -> 51.4 us
    pallas_call x1, Pallas kernels: 53.3 us -> 51.4 us  [local(): pl.pallas_call(functools.partial(kernel, groups), out_shape=pltpu.VMEM((S...]
where the time goes in v5:
time: 52.2 us; the launch traced here: 52 us
  Pallas kernels  51.4 us (98%)
  local copies, waits for them, and re-layouts  0.58 us (1%)
    pallas_call x1, Pallas kernels, local(): pl.pallas_call(functools.partial(kernel, groups), out_shape=pltpu.VMEM((S...  51.4 us

profile of v5, /device:TPU:1, one launch (start us, length us, event | category | flops | bytes accessed | tf_op | source)
XLA Modules:
  0.0 52.0 jit_solution(15412990302126206103)
XLA Ops:
  0.0 51.4 %shard_map.82 = f32[4,12]{1,0:T(4,128)S(1)} custom-call(f32[3,4,4096]{2,1,0:T(4,128)} %bitcast.6, f32[192,128]{1,0:T(8,128)} %bitcast.7, f32[12,1024]{1,0:T(8,128)} %poses_hbm.1, f32[4]{0:T(128)} %anchor_ref.1, s32[4,4]{1,0:T(4,128)} %target_ref.1, s32[4,4,4]{2,1,0:T(4,128)} %tile_ref.1, s32[4,4,4,128]{3,2,1,0:T(4,128)} %corr_source_hbm.1, ...), custom_call_target="tpu_custom_call" | custom-call | tf_op jit(solution)/shard_map/pallas_call | solution.py:616
  51.4 0.6 %copy.10 = f32[12,4]{0,1:T(4,128)} copy(f32[12,4]{0,1:T(4,128)S(1)} %bitcast.5) | data formatting | bytes 384

commit v6 on v5

--- a/solution.py
+++ b/solution.py
@@ -40,6 +40,25 @@
 
 def dot(a, b):
     return jnp.dot(a, b, preferred_element_type=F32)
+
+
+def moved_pose(pose, inc):
+    turn_mat = cayley(0.5 * inc[0], 0.5 * inc[1], 0.5 * inc[2])
+    rotated = [
+        turn_mat[3 * i] * pose[j]
+        + turn_mat[3 * i + 1] * pose[3 + j]
+        + turn_mat[3 * i + 2] * pose[6 + j]
+        for i in range(3)
+        for j in range(3)
+    ]
+    moved = [
+        turn_mat[3 * i] * pose[9]
+        + turn_mat[3 * i + 1] * pose[10]
+        + turn_mat[3 * i + 2] * pose[11]
+        + inc[3 + i]
+        for i in range(3)
+    ]
+    return rotated + moved
 
 
 def rows_times(value, select):
@@ -194,7 +213,16 @@
         for device in devices:
             pl.semaphore_signal(semaphore, inc=1, device_id=device, device_id_type=MESH)
 
-    greeted = [device for device, _ in halo_partners] + z_line + y_line + x_line
+    chain_line = []
+    for offset in (1, -1, 2, -2, 3, -3):
+        inside = (sub_low + offset + half_groups) // half_groups
+        crosses = lax.bitwise_xor(inside, 1)
+        flip = 2 * jnp.minimum(crosses, 1)
+        chain_line.append((near_by(offset), lax.bitwise_xor(dom, flip)))
+        if abs(offset) == 1:
+            chain_line.append((near_by(offset), lax.bitwise_xor(dom, 2 - flip)))
+    group_line = [(sub, lax.bitwise_xor(dom, other)) for other in (1, 2, 3)]
+    greeted = chain_line + group_line + z_line + y_line + x_line
     signal_all(barrier, greeted)
 
     pl.semaphore_wait(barrier, len(greeted))
@@ -274,6 +302,9 @@
     for part in range(PARTS):
         window_send(0, part, 4 + dom, (near_by(1), to_next), dom)
         window_send(1, part, 4 + dom, (near_by(-1), to_last), 8 + dom)
+    for part in range(1, PARTS):
+        window_send(4, part, 4 + dom, (near_by(1), lax.bitwise_xor(to_next, 2)), dom)
+        window_send(5, part, 4 + dom, (near_by(-1), lax.bitwise_xor(to_last, 2)), 8 + dom)
     for part in range(PARTS):
         window_send(2, part, 4 + dom, to_across)
     for part in range(PARTS):
@@ -289,8 +320,10 @@
     for scan in range(SCAN_DEV):
         row = jnp.where(lane_row == EDGES + scan, anchor_ref[scan], row)
     early[pl.ds(own_slot, 1)] = row.reshape(1, 1, 128)
+    signal_all(word.at[0], y_line)
+    signal_all(word.at[2], group_line)
+    pl.semaphore_wait(word.at[2], len(group_line))
     early_copies = halo_push(early, 1, early_send, early_recv)
-    signal_all(word.at[0], y_line)
     started.append(early_copies)
     early[pl.ds(TILES, 4)] = jnp.zeros((4, 1, 128), F32)
     for step in range(GN_ITERS):
@@ -326,7 +359,8 @@
         gather_scan(part)
         for number, slot in ((4, to_last), (5, 8 + to_next)):
             window_wait(part, slot)
-            window_send(number, part, slot, to_across)
+            if part == 0:
+                window_send(number, part, slot, to_across)
             window_send(number + 2, part, slot, to_sibling)
         window_wait(part, 4 + across)
         window_send(8, part, 4 + across, to_sibling)
@@ -370,51 +404,20 @@
     row_of = iota((16, 6 * 128), 0) == lax.shift_right_logical(iota((16, 6 * 128), 1), 7)
     into_rows = jnp.where(row_of, 1.0, 0.0).astype(BF16)
 
-    early_copies.wait_recv()
-    rows = early[...].reshape(PAD, 128)
-    rows_turned = jnp.concatenate([rows, jnp.zeros((128 - PAD, 128), F32)], axis=0).T
+    pose_rows = jnp.concatenate(pose + [jnp.zeros((4, 128), F32)], axis=0)
+    pose_ends = pick_turned(own_ends, pose_rows)
+    end_poses = [
+        [
+            jnp.broadcast_to(
+                pose_ends[end * EDGES : (end + 1) * EDGES, k : k + 1], (EDGES, 128)
+            )
+            for k in range(12)
+        ]
+        for end in range(2)
+    ]
+
     lane8 = iota((8, 128), 1)
     row8 = iota((8, 128), 0)
-    for tile in range(TILES):
-        target = rows_turned[:EDGES, tile : tile + 1]
-        target_lane = target + float((tile // 4 - 1) * 16)
-        source_lane = tile * 4 + edge_of_row // EDGE_SCAN
-        ends[pl.ds(tile * EDGES, EDGES), :] = (lane16 == source_lane).astype(F32) - (
-            lane16.astype(F32) == target_lane
-        ).astype(F32)
-    ends[pl.ds(TILES * EDGES, (PAD - TILES) * EDGES), :] = jnp.zeros(
-        ((PAD - TILES) * EDGES, 128), F32
-    )
-    ends_f32 = ends[...]
-    ends_out = ends_f32.astype(BF16)
-    ends_abs = jnp.abs(ends_f32).astype(BF16)
-    node_of = iota((128, PAD * EDGES), 0)
-    ends_turned = ends_f32.T
-    far_end = jnp.sum(
-        jnp.where(ends_turned < 0.0, node_of, 0), axis=0, keepdims=True
-    )
-    near_lanes = []
-    far_lanes = []
-    for group in range(PAD // 8):
-        near_lanes.append(group * 32 + lane8 // EDGE_SCAN)
-        far_lanes.append(
-            jnp.broadcast_to(far_end[:, group * 128 : group * 128 + 128], (8, 128))
-        )
-
-    def along_edges(value, group):
-        near = jnp.take_along_axis(value, near_lanes[group], axis=1, mode="promise_in_bounds")
-        far_value = jnp.take_along_axis(
-            value, far_lanes[group], axis=1, mode="promise_in_bounds"
-        )
-        return near - far_value
-
-    of_tile = jnp.where(iota((128, 128), 0) == iota((128, 128), 1) // 4, 1.0, 0.0).astype(BF16)
-    anchor_rows = rows_times(rows_turned[EDGES : EDGES + 8], of_tile)
-    anchor = jnp.sum(
-        jnp.where(row8 == lax.bitwise_and(lane8, 3), anchor_rows, 0.0), axis=0, keepdims=True
-    )
-    anchor = jnp.broadcast_to(anchor, (8, 128))
-    anchor = jnp.where(lane8 < TILES * 4, anchor, 1.0)
     for part in range(PARTS):
         for other in (sibling, lax.bitwise_xor(dom, 3)):
             for offset in range(3):
@@ -443,14 +446,7 @@
 
 
     for step in range(GN_ITERS):
-        pose_rows = jnp.concatenate(pose + [jnp.zeros((4, 128), F32)], axis=0)
-        pose_ends = pick_turned(own_ends, pose_rows)
-        here = [
-            jnp.broadcast_to(pose_ends[:EDGES, k : k + 1], (EDGES, 128)) for k in range(12)
-        ]
-        there = [
-            jnp.broadcast_to(pose_ends[EDGES:, k : k + 1], (EDGES, 128)) for k in range(12)
-        ]
+        here, there = end_poses
         sums = {}
         for chunk in range(CT):
             data = [comps[k, chunk] for k in range(9)]
@@ -501,7 +497,55 @@
         message = message[:8] * (1.0 / SAMPLES)
         gram[step, pl.ds(own_slot, 1)] = message.reshape(1, 8, 128)
         gram_copies = halo_push(gram.at[step], 6, gram_send.at[step], gram_recv.at[step])
-        started.append(gram_copies)
+        if step == 0:
+            for copy in started:
+                copy.wait_send()
+            started = []
+            early_copies.wait_recv()
+            rows = early[...].reshape(PAD, 128)
+            rows_turned = jnp.concatenate([rows, jnp.zeros((128 - PAD, 128), F32)], axis=0).T
+            lane8 = iota((8, 128), 1)
+            row8 = iota((8, 128), 0)
+            for tile in range(TILES):
+                target = rows_turned[:EDGES, tile : tile + 1]
+                target_lane = target + float((tile // 4 - 1) * 16)
+                source_lane = tile * 4 + edge_of_row // EDGE_SCAN
+                ends[pl.ds(tile * EDGES, EDGES), :] = (lane16 == source_lane).astype(F32) - (
+                    lane16.astype(F32) == target_lane
+                ).astype(F32)
+            ends[pl.ds(TILES * EDGES, (PAD - TILES) * EDGES), :] = jnp.zeros(
+                ((PAD - TILES) * EDGES, 128), F32
+            )
+            ends_f32 = ends[...]
+            ends_out = ends_f32.astype(BF16)
+            ends_abs = jnp.abs(ends_f32).astype(BF16)
+            node_of = iota((128, PAD * EDGES), 0)
+            ends_turned = ends_f32.T
+            far_end = jnp.sum(
+                jnp.where(ends_turned < 0.0, node_of, 0), axis=0, keepdims=True
+            )
+            near_lanes = []
+            far_lanes = []
+            for group in range(PAD // 8):
+                near_lanes.append(group * 32 + lane8 // EDGE_SCAN)
+                far_lanes.append(
+                    jnp.broadcast_to(far_end[:, group * 128 : group * 128 + 128], (8, 128))
+                )
+
+            def along_edges(value, group):
+                near = jnp.take_along_axis(value, near_lanes[group], axis=1, mode="promise_in_bounds")
+                far_value = jnp.take_along_axis(
+                    value, far_lanes[group], axis=1, mode="promise_in_bounds"
+                )
+                return near - far_value
+
+            of_tile = jnp.where(iota((128, 128), 0) == iota((128, 128), 1) // 4, 1.0, 0.0).astype(BF16)
+            anchor_rows = rows_times(rows_turned[EDGES : EDGES + 8], of_tile)
+            anchor = jnp.sum(
+                jnp.where(row8 == lax.bitwise_and(lane8, 3), anchor_rows, 0.0), axis=0, keepdims=True
+            )
+            anchor = jnp.broadcast_to(anchor, (8, 128))
+            anchor = jnp.where(lane8 < TILES * 4, anchor, 1.0)
         gram_copies.wait_recv()
         tiles = gram[step]
         grouped = [regroup([tiles[8 * g + t] for t in range(8)]) for g in range(PAD // 8)]
@@ -545,24 +589,36 @@
         )
         sums_row = jnp.sum(jnp.where(row8 < 6, packed, 0.0), axis=0, keepdims=True)
 
-        def exchange(value, buffer, spot, count, send, recv, partners):
-            buffer[step, pl.ds(spot, 1)] = value.reshape(1, 1, 128)
-            own = buffer.at[step, pl.ds(spot, 1)]
-            push(
-                [(own, buffer.at[step, pl.ds(at, 1)], device) for device, at in partners],
-                send.at[step],
-                recv.at[step],
-            )
-            others = whole(
-                buffer.at[step, pl.ds(0, count - 1)], send.at[step], recv.at[step]
-            )
-            others.wait_recv()
-            started.append(others)
-            return jnp.sum(buffer[step].reshape(count, 128), axis=0, keepdims=True)
-
-        sums_row = exchange(
-            sums_row, far, sub, groups, far_send, far_recv, sum_partners
-        )
+        far[step, pl.ds(sub, 1)] = sums_row.reshape(1, 1, 128)
+        own_sum = far.at[step, pl.ds(sub, 1)]
+        push(
+            [(own_sum, far.at[step, pl.ds(at, 1)], device) for device, at in sum_partners],
+            far_send.at[step],
+            far_recv.at[step],
+        )
+        sum_copies = whole(
+            far.at[step, pl.ds(0, groups - 1)], far_send.at[step], far_recv.at[step]
+        )
+        gram_copies.wait_send()
+        if step + 1 < GN_ITERS:
+            both = pick_turned(own_ends, jnp.concatenate([scaled, second], axis=0))
+            first_ends, second_ends = [
+                [
+                    [
+                        jnp.broadcast_to(
+                            both[end * EDGES : (end + 1) * EDGES, at + k : at + k + 1],
+                            (EDGES, 128),
+                        )
+                        for k in range(6)
+                    ]
+                    for end in range(2)
+                ]
+                for at in (0, 8)
+            ]
+        sum_copies.wait_recv()
+        started.append(sum_copies)
+        sums_row = jnp.sum(far[step].reshape(groups, 128), axis=0, keepdims=True)
+
         part_of = jnp.minimum(lane_row // 16, 3)
         energy, curve, cross, bend = [
             jnp.sum(jnp.where(part_of == k, sums_row, 0.0), axis=1, keepdims=True)
@@ -579,26 +635,21 @@
             + ratio * ratio * curve
         )
         step_two = renewed / curve_two
-        increment = (step_one + step_two * (1.0 + ratio)) * scaled - (
-            step_two * step_one
-        ) * second
-        inc = [increment[k : k + 1] for k in range(6)]
-        turn_mat = cayley(0.5 * inc[0], 0.5 * inc[1], 0.5 * inc[2])
-        rotated = [
-            turn_mat[3 * i] * pose[j]
-            + turn_mat[3 * i + 1] * pose[3 + j]
-            + turn_mat[3 * i + 2] * pose[6 + j]
-            for i in range(3)
-            for j in range(3)
-        ]
-        moved = [
-            turn_mat[3 * i] * pose[9]
-            + turn_mat[3 * i + 1] * pose[10]
-            + turn_mat[3 * i + 2] * pose[11]
-            + inc[3 + i]
-            for i in range(3)
-        ]
-        pose = rotated + moved
+        first_factor = step_one + step_two * (1.0 + ratio)
+        second_factor = -step_two * step_one
+        increment = first_factor * scaled + second_factor * second
+        pose = moved_pose(pose, [increment[k : k + 1] for k in range(6)])
+        if step + 1 < GN_ITERS:
+            end_poses = [
+                moved_pose(
+                    end_poses[end],
+                    [
+                        first_factor * first_ends[end][k] + second_factor * second_ends[end][k]
+                        for k in range(6)
+                    ],
+                )
+                for end in range(2)
+            ]
 
     final = jnp.concatenate(pose + [jnp.zeros((4, 128), F32)], axis=0)
     final = pltpu.roll(final, 128 - (REACH * 16 + dom * SCAN_DEV), 1)
@@ -640,7 +691,7 @@
             dma((GN_ITERS,)),
             dma((GN_ITERS,)),
             dma((5,)),
-            pltpu.SemaphoreType.REGULAR((2,)),
+            pltpu.SemaphoreType.REGULAR((3,)),
         ],
         compiler_params=pltpu.CompilerParams(collective_id=0, has_side_effects=True),
     )(

time: 52.2 us -> 50.9 us (0.975)
  Pallas kernels: 51.4 us -> 50.2 us
    pallas_call x1, Pallas kernels: 51.4 us -> 50.2 us  [local(): pl.pallas_call(functools.partial(kernel, groups), out_shape=pltpu.VMEM((S...]
where the time goes in v6:
time: 50.9 us; the launch traced here: 50.8 us
  Pallas kernels  50.2 us (99%)
  local copies, waits for them, and re-layouts  0.58 us (1%)
    pallas_call x1, Pallas kernels, local(): pl.pallas_call(functools.partial(kernel, groups), out_shape=pltpu.VMEM((S...  50.2 us

profile of v6, /device:TPU:1, one launch (start us, length us, event | category | flops | bytes accessed | tf_op | source)
XLA Modules:
  0.0 50.8 jit_solution(1126908648308281918)
XLA Ops:
  0.0 50.2 %shard_map.82 = f32[4,12]{1,0:T(4,128)S(1)} custom-call(f32[3,4,4096]{2,1,0:T(4,128)} %bitcast.6, f32[192,128]{1,0:T(8,128)} %bitcast.7, f32[12,1024]{1,0:T(8,128)} %poses_hbm.1, f32[4]{0:T(128)} %anchor_ref.1, s32[4,4]{1,0:T(4,128)} %target_ref.1, s32[4,4,4]{2,1,0:T(4,128)} %tile_ref.1, s32[4,4,4,128]{3,2,1,0:T(4,128)} %corr_source_hbm.1, ...), custom_call_target="tpu_custom_call" | custom-call | tf_op jit(solution)/shard_map/pallas_call | solution.py:667
  50.2 0.6 %copy.10 = f32[12,4]{0,1:T(4,128)} copy(f32[12,4]{0,1:T(4,128)S(1)} %bitcast.5) | data formatting | bytes 384

commit v7 on v6

--- a/solution.py
+++ b/solution.py
@@ -114,12 +114,15 @@
     source_hbm,
     boundary_hbm,
     poses_hbm,
+    anchor_hbm,
+    target_hbm,
+    tile_hbm,
+    corr_source_hbm,
+    corr_lane_hbm,
+    out_ref,
     anchor_ref,
     target_ref,
     tile_ref,
-    corr_source_hbm,
-    corr_lane_hbm,
-    out_ref,
     corr_source_ref,
     corr_lane_ref,
     source_ref,
@@ -191,6 +194,9 @@
                 (source_hbm, source_ref),
                 (poses_hbm, poses_ref),
                 (corr_lane_hbm, corr_lane_ref),
+                (anchor_hbm, anchor_ref),
+                (target_hbm, target_ref),
+                (tile_hbm, tile_ref),
             )
         )
     ]
@@ -309,6 +315,8 @@
         window_send(2, part, 4 + dom, to_across)
     for part in range(PARTS):
         window_send(3, part, 4 + dom, to_sibling)
+    for number in (5, 6, 7):
+        loads[number].wait()
     lane_row = iota((1, 128), 1)
     row = jnp.zeros((1, 128), F32)
     edge_of_row = iota((EDGES, 128), 0)
@@ -661,15 +669,17 @@
 
 def local(groups, source_points, boundary, poses, anchor, edge_target, corr_tile, corr_source, corr_lane):
     vmem = pl.BlockSpec(memory_space=pltpu.VMEM)
-    smem = pl.BlockSpec(memory_space=pltpu.SMEM)
     hbm = pl.BlockSpec(memory_space=pl.ANY)
     dma = pltpu.SemaphoreType.DMA
     return pl.pallas_call(
         functools.partial(kernel, groups),
         out_shape=pltpu.VMEM((SCAN_DEV, 12), F32),
-        in_specs=[hbm, hbm, hbm, smem, smem, smem, hbm, hbm],
+        in_specs=[hbm] * 8,
         out_specs=vmem,
         scratch_shapes=[
+            pltpu.SMEM(anchor.shape, F32),
+            pltpu.SMEM(edge_target.shape, jnp.int32),
+            pltpu.SMEM(corr_tile.shape, jnp.int32),
             pltpu.VMEM(corr_source.shape, jnp.int32),
             pltpu.VMEM(corr_lane.shape, jnp.int32),
             pltpu.VMEM((3, SCAN_DEV, source_points.shape[2]), F32),
@@ -690,7 +700,7 @@
             dma((GN_ITERS,)),
             dma((GN_ITERS,)),
             dma((GN_ITERS,)),
-            dma((5,)),
+            dma((8,)),
             pltpu.SemaphoreType.REGULAR((3,)),
         ],
         compiler_params=pltpu.CompilerParams(collective_id=0, has_side_effects=True),

time: 50.9 us -> 49.9 us (0.980)
  Pallas kernels: 50.2 us -> 49.3 us
    pallas_call x1, Pallas kernels: 50.2 us -> 49.3 us  [local(): pl.pallas_call(functools.partial(kernel, groups), out_shape=pltpu.VMEM((S...]
where the time goes in v7:
time: 49.9 us
  Pallas kernels  49.3 us (99%)
  local copies, waits for them, and re-layouts  0.58 us (1%)
    pallas_call x1, Pallas kernels, local(): pl.pallas_call(functools.partial(kernel, groups), out_shape=pltpu.VMEM((S...  49.3 us

profile of v7, /device:TPU:1, one launch (start us, length us, event | category | flops | bytes accessed | tf_op | source)
XLA Modules:
  0.0 49.9 jit_solution(4174738493294325174)
XLA Ops:
  0.0 49.3 %shard_map.82 = f32[4,12]{1,0:T(4,128)S(1)} custom-call(f32[3,4,4096]{2,1,0:T(4,128)} %bitcast.6, f32[192,128]{1,0:T(8,128)} %bitcast.7, f32[12,1024]{1,0:T(8,128)} %poses_hbm.1, f32[4]{0:T(128)} %anchor_hbm.1, s32[4,4]{1,0:T(4,128)} %target_hbm.1, s32[4,4,4]{2,1,0:T(4,128)} %tile_hbm.1, s32[4,4,4,128]{3,2,1,0:T(4,128)} %corr_source_hbm.1, ...), custom_call_target="tpu_custom_call" | custom-call | tf_op jit(solution)/shard_map/pallas_call | solution.py:674
  49.3 0.6 %copy.10 = f32[12,4]{0,1:T(4,128)} copy(f32[12,4]{0,1:T(4,128)S(1)} %bitcast.5) | data formatting | bytes 384

commit v8 on v7

--- a/solution.py
+++ b/solution.py
@@ -306,15 +306,14 @@
         window_copy(0, part, slot, to_sibling).wait_recv()
 
     for part in range(PARTS):
+        window_send(2, part, 4 + dom, to_across)
+        window_send(3, part, 4 + dom, to_sibling)
+    for part in range(PARTS):
         window_send(0, part, 4 + dom, (near_by(1), to_next), dom)
         window_send(1, part, 4 + dom, (near_by(-1), to_last), 8 + dom)
     for part in range(1, PARTS):
         window_send(4, part, 4 + dom, (near_by(1), lax.bitwise_xor(to_next, 2)), dom)
         window_send(5, part, 4 + dom, (near_by(-1), lax.bitwise_xor(to_last, 2)), 8 + dom)
-    for part in range(PARTS):
-        window_send(2, part, 4 + dom, to_across)
-    for part in range(PARTS):
-        window_send(3, part, 4 + dom, to_sibling)
     for number in (5, 6, 7):
         loads[number].wait()
     lane_row = iota((1, 128), 1)
@@ -365,13 +364,13 @@
     loads[2].wait()
     for part in range(PARTS):
         gather_scan(part)
+        window_wait(part, 4 + across)
+        window_send(8, part, 4 + across, to_sibling)
         for number, slot in ((4, to_last), (5, 8 + to_next)):
             window_wait(part, slot)
             if part == 0:
                 window_send(number, part, slot, to_across)
             window_send(number + 2, part, slot, to_sibling)
-        window_wait(part, 4 + across)
-        window_send(8, part, 4 + across, to_sibling)
     pl.semaphore_wait(word.at[0], len(y_line))
     signal_all(word.at[1], x_line)
     gather_scan(2)
@@ -684,12 +683,12 @@
             pltpu.VMEM(corr_lane.shape, jnp.int32),
             pltpu.VMEM((3, SCAN_DEV, source_points.shape[2]), F32),
             pltpu.VMEM(poses.shape, F32),
-            pltpu.VMEM((12 * ROWS + 16, 128), F32),
+            pltpu.VMEM((12 * ROWS + 64, 128), F32),
             pltpu.VMEM((PAD, 1, 128), F32),
             pltpu.VMEM((GN_ITERS, PAD, 8, 128), F32),
             pltpu.VMEM((GN_ITERS, groups, 1, 128), F32),
-            pltpu.VMEM((3, 64, 128), F32),
-            pltpu.VMEM((512, 128), F32),
+            pltpu.VMEM((3, 72, 128), F32),
+            pltpu.VMEM((544, 128), F32),
             pltpu.VMEM((9, CT, EDGES, 128), F32),
             pltpu.VMEM((PAD * EDGES, 128), F32),
             dma((11, PARTS)),

time: 49.9 us -> 49.9 us (level)
  no operation moved by 1% of the time
where the time goes in v8:
time: 49.9 us
  Pallas kernels  49.3 us (99%)
  local copies, waits for them, and re-layouts  0.58 us (1%)
    pallas_call x1, Pallas kernels, local(): pl.pallas_call(functools.partial(kernel, groups), out_shape=pltpu.VMEM((S...  49.3 us

profile of v8, /device:TPU:1, one launch (start us, length us, event | category | flops | bytes accessed | tf_op | source)
XLA Modules:
  0.0 49.9 jit_solution(13349889579442677981)
XLA Ops:
  0.0 49.3 %shard_map.82 = f32[4,12]{1,0:T(4,128)S(1)} custom-call(f32[3,4,4096]{2,1,0:T(4,128)} %bitcast.6, f32[192,128]{1,0:T(8,128)} %bitcast.7, f32[12,1024]{1,0:T(8,128)} %poses_hbm.1, f32[4]{0:T(128)} %anchor_hbm.1, s32[4,4]{1,0:T(4,128)} %target_hbm.1, s32[4,4,4]{2,1,0:T(4,128)} %tile_hbm.1, s32[4,4,4,128]{3,2,1,0:T(4,128)} %corr_source_hbm.1, ...), custom_call_target="tpu_custom_call" | custom-call | tf_op jit(solution)/shard_map/pallas_call | solution.py:673
  49.3 0.6 %copy.10 = f32[12,4]{0,1:T(4,128)} copy(f32[12,4]{0,1:T(4,128)S(1)} %bitcast.5) | data formatting | bytes 384

commit v9 on v8

--- a/solution.py
+++ b/solution.py
@@ -62,9 +62,9 @@
 
 
 def rows_times(value, select):
-    stacked = jnp.concatenate([part.astype(F32) for part in parts_of(value, 3)], axis=0)
+    stacked = jnp.concatenate([part.astype(F32) for part in parts_of(value)], axis=0)
     product = dot(stacked.astype(BF16), select)
-    return (product[0:8] + product[8:16]) + product[16:24]
+    return product[0:8] + product[8:16]
 
 
 def regroup(tiles):

time: 49.9 us -> 49.9 us (level)
  no operation moved by 1% of the time
where the time goes in v9:
time: 49.9 us; the launch traced here: 49.8 us
  Pallas kernels  49.2 us (99%)
  local copies, waits for them, and re-layouts  0.58 us (1%)
    pallas_call x1, Pallas kernels, local(): pl.pallas_call(functools.partial(kernel, groups), out_shape=pltpu.VMEM((S...  49.2 us

profile of v9, /device:TPU:1, one launch (start us, length us, event | category | flops | bytes accessed | tf_op | source)
XLA Modules:
  0.0 49.8 jit_solution(446830749199995981)
XLA Ops:
  0.0 49.2 %shard_map.82 = f32[4,12]{1,0:T(4,128)S(1)} custom-call(f32[3,4,4096]{2,1,0:T(4,128)} %bitcast.6, f32[192,128]{1,0:T(8,128)} %bitcast.7, f32[12,1024]{1,0:T(8,128)} %poses_hbm.1, f32[4]{0:T(128)} %anchor_hbm.1, s32[4,4]{1,0:T(4,128)} %target_hbm.1, s32[4,4,4]{2,1,0:T(4,128)} %tile_hbm.1, s32[4,4,4,128]{3,2,1,0:T(4,128)} %corr_source_hbm.1, ...), custom_call_target="tpu_custom_call" | custom-call | tf_op jit(solution)/shard_map/pallas_call | solution.py:673
  49.2 0.6 %copy.10 = f32[12,4]{0,1:T(4,128)} copy(f32[12,4]{0,1:T(4,128)S(1)} %bitcast.5) | data formatting | bytes 384
